TPU v7x, 128 devices: a whole 4x4x4 slice. The times are simulated.
128 devices in a mesh: pipe: 4 (over z), head: 32 (over y, x, core).
Axes of the slice: x: 4, y: 4, z: 4, core: 2. Of those that a mesh axis runs over, the one named last changes fastest.
Arguments:
- hidden: bfloat16 [2, 64, 8192], P(None, 'head'), may hold values from -6 to 6
- norm_gain: float32 [4, 8192], P('pipe'), may hold values from 0.1 to 1.9
- w_x: bfloat16 [4, 8192, 16384], P('pipe', None, 'head'), may hold values from -0.0625 to 0.0625
- w_bc: bfloat16 [4, 8192, 4096], P('pipe', None, 'head'), may hold values from -0.03125 to 0.03125
- w_dt: bfloat16 [4, 8192, 256], P('pipe', None, 'head'), may hold values from -0.0625 to 0.0625
- conv_x: float32 [4, 4, 16384], P('pipe', None, 'head'), may hold values from -3 to 3
- conv_bc: float32 [4, 4, 4096], P('pipe'), may hold values from -3 to 3
- dt_bias: float32 [4, 256], P('pipe', 'head'), may hold values from -3 to 0.5
- a_rate: float32 [4, 256], P('pipe', 'head'), may hold values from 0.002 to 0.2
- d_skip: float32 [4, 256], P('pipe', 'head'), may hold values from 0.5 to 1.5
- w_out: bfloat16 [4, 16384, 8192], P('pipe', 'head'), may hold values from -0.046875 to 0.046875
- ssm_init: float32 [4, 256, 64, 256], P('pipe', 'head'), may hold values from -0.6 to 0.6
- conv_x_init: float32 [4, 3, 16384], P('pipe', None, 'head'), may hold values from -6 to 6
- conv_bc_init: float32 [4, 3, 4096], P('pipe'), may hold values from -3 to 3
Outputs:
- segment_out: bfloat16 [4, 2, 64, 8192], P('pipe', None, 'head')
- state_out: float32 [4, 256, 64, 256], P('pipe', 'head')
All inputs are finite; a program needn't handle non-finite values.
Results may differ from a plain program's by a relative error of at most 0.039.
Values may be sent and summed in bfloat16 or wider, within the bound.
A program may use at most 128 MiB of HBM per device.

v0:
```python
import jax
import jax.numpy as jnp
from jax import lax
from jax.sharding import PartitionSpec as P

HEADS = 256
STATE = 256
GROUPS = 8


def passed_along(value, axis, steps):
    count = lax.axis_size(axis)
    initial, last = (max(0, -steps), min(count, count - steps))
    return lax.ppermute(value, axis, [(source, source + steps) for source in range(initial, last)])


def rms_rows(block_in, norm_weight):
    floats = block_in.astype(jnp.float32)
    scaled = floats * lax.rsqrt(jnp.mean(floats * floats, axis=-1, keepdims=True) + 1e-05)
    return (scaled * norm_weight[None, :]).astype(jnp.bfloat16)


def causal_conv(tail_rows, values, taps):
    padded = jnp.concatenate([tail_rows, values], axis=0)
    length = values.shape[0]
    conv_sum = taps[0][None, :] * padded[0:length]
    for offset in range(1, taps.shape[0]):
        conv_sum = conv_sum + taps[offset][None, :] * padded[offset : offset + length]
    return (jax.nn.silu(conv_sum), padded[length:])


def scan_block(values, b_heads, c_heads, step_size, decay_rate, skip_gain, ssm_state):
    highest = lax.Precision.HIGHEST
    log_decay = jnp.cumsum(-step_size * decay_rate[None, :], axis=0)
    length = values.shape[0]
    causal = (jnp.arange(length)[:, None] >= jnp.arange(length)[None, :])[:, :, None]
    gap_log = log_decay[:, None, :] - log_decay[None, :, :]
    decay_pairs = jnp.where(causal, jnp.exp(jnp.where(causal, gap_log, 0.0)), 0.0)
    scores = jnp.einsum("thn,shn->tsh", c_heads, b_heads, precision=highest)
    pair_weight = scores * decay_pairs * step_size[None, :, :]
    within = jnp.einsum("tsh,shp->thp", pair_weight, values, precision=highest)
    carried = jnp.exp(log_decay)[:, :, None] * jnp.einsum(
        "thn,hpn->thp", c_heads, ssm_state, precision=highest
    )
    mixed_out = within + carried + skip_gain[None, :, None] * values
    end_log = log_decay[-1]
    to_end = jnp.exp(end_log[None, :] - log_decay) * step_size
    new_state = jnp.exp(end_log)[:, None, None] * ssm_state + jnp.einsum(
        "sh,shp,shn->hpn", to_end, values, b_heads, precision=highest
    )
    return (mixed_out, new_state)


def mix_block(
    block_in,
    norm_weight,
    proj_x,
    proj_bc,
    proj_dt,
    taps_x,
    taps_bc,
    step_bias,
    decay_rate,
    skip_gain,
    ssm_state,
    tail_x,
    tail_bc,
    group_pick,
):
    highest = lax.Precision.HIGHEST
    normed = rms_rows(block_in, norm_weight)
    x_proj = jnp.dot(normed, proj_x, preferred_element_type=jnp.float32)
    bc_part = jnp.dot(normed, proj_bc, preferred_element_type=jnp.float32).astype(jnp.bfloat16)
    bc_all = lax.all_gather(bc_part, "head", axis=1, tiled=True)
    dt_raw = jnp.dot(normed, proj_dt, preferred_element_type=jnp.float32)
    x_conv, new_tail_x = causal_conv(tail_x, x_proj, taps_x)
    bc_conv, new_tail_bc = causal_conv(tail_bc, bc_all.astype(jnp.float32), taps_bc)
    length = block_in.shape[0]
    grouped = bc_conv.reshape(length, 2, STATE, GROUPS)
    b_heads = jnp.einsum("tng,hg->thn", grouped[:, 0], group_pick, precision=highest)
    c_heads = jnp.einsum("tng,hg->thn", grouped[:, 1], group_pick, precision=highest)
    step_size = jax.nn.softplus(dt_raw + step_bias[None, :])
    local_heads = step_bias.shape[0]
    mixed, new_state = scan_block(
        x_conv.reshape(length, local_heads, -1),
        b_heads,
        c_heads,
        step_size,
        decay_rate,
        skip_gain,
        ssm_state,
    )
    return (mixed.reshape(length, -1).astype(jnp.bfloat16), new_state, new_tail_x, new_tail_bc)


def per_device(
    hidden,
    norm_gain,
    w_x,
    w_bc,
    w_dt,
    conv_x,
    conv_bc,
    dt_bias,
    a_rate,
    d_skip,
    w_out,
    ssm_init,
    conv_x_init,
    conv_bc_init,
):
    segment_index = lax.axis_index("pipe")
    pipe_count = lax.axis_size("pipe")
    head_index = lax.axis_index("head")
    head_count = lax.axis_size("head")
    micro_count, local_rows, model_width = hidden.shape
    block_rows = local_rows * head_count
    local_heads = dt_bias.shape[1]
    global_heads = head_index * local_heads + jnp.arange(local_heads)
    group_pick = (global_heads[:, None] // (HEADS // GROUPS) == jnp.arange(GROUPS)[None, :]).astype(
        jnp.float32
    )
    out_weight = w_out[0]
    ssm_state = ssm_init[0]
    tail_x = conv_x_init[0]
    tail_bc = conv_bc_init[0]
    out_rows = jnp.zeros((micro_count, local_rows, model_width), jnp.bfloat16)
    recv_full = jnp.zeros((block_rows, model_width), jnp.bfloat16)
    for tick_number in range(micro_count + pipe_count - 1):
        position = tick_number - segment_index
        active = jnp.logical_and(position >= 0, position < micro_count)
        clamped = jnp.clip(position, 0, micro_count - 1)
        own_rows = lax.dynamic_index_in_dim(hidden, clamped, 0, keepdims=False)
        entry_rows = lax.all_gather(own_rows, "head", axis=0, tiled=True)
        block_in = jnp.where(segment_index == 0, entry_rows, recv_full)
        mixed_bf, new_state, new_tail_x, new_tail_bc = mix_block(
            block_in,
            norm_gain[0],
            w_x[0],
            w_bc[0],
            w_dt[0],
            conv_x[0],
            conv_bc[0],
            dt_bias[0],
            a_rate[0],
            d_skip[0],
            ssm_state,
            tail_x,
            tail_bc,
            group_pick,
        )
        summed = lax.psum(
            jnp.dot(mixed_bf, out_weight, preferred_element_type=jnp.float32).astype(jnp.bfloat16),
            "head",
        ).astype(jnp.float32)
        new_full = (block_in.astype(jnp.float32) + summed).astype(jnp.bfloat16)
        new_rows = lax.dynamic_slice_in_dim(new_full, head_index * local_rows, local_rows, 0)
        recv_full = passed_along(new_full, "pipe", 1)
        ssm_state = jnp.where(active, new_state, ssm_state)
        tail_x = jnp.where(active, new_tail_x, tail_x)
        tail_bc = jnp.where(active, new_tail_bc, tail_bc)
        current = lax.dynamic_index_in_dim(out_rows, clamped, 0, keepdims=False)
        out_rows = lax.dynamic_update_index_in_dim(
            out_rows, jnp.where(active, new_rows, current), clamped, 0
        )
    return (out_rows[None], ssm_state[None])


def solution(mesh):
    in_specs = (
        P(None, "head", None),
        P("pipe", None),
        P("pipe", None, "head"),
        P("pipe", None, "head"),
        P("pipe", None, "head"),
        P("pipe", None, "head"),
        P("pipe", None, None),
        P("pipe", "head"),
        P("pipe", "head"),
        P("pipe", "head"),
        P("pipe", "head", None),
        P("pipe", "head", None, None),
        P("pipe", None, "head"),
        P("pipe", None, None),
    )
    out_specs = (P("pipe", None, "head", None), P("pipe", "head", None, None))
    return jax.shard_map(
        per_device, mesh=mesh, in_specs=in_specs, out_specs=out_specs, check_vma=False
    )
```

profile of v0, /device:TPU:97, one launch (start us, length us, event | category | flops | bytes accessed | tf_op | source)
XLA Modules:
  0.0 1089.6 jit_solution(12420424981830480195)
XLA Ops:
  13.8 42.5 %all-gather.11.cloned.1.call-done = bf16[1,64,8192]{2,0,1:T(2,128)(2,1)} async-done(((bf16[1,2,8192]{2,0,1:T(2,128)(2,1)}), bf16[1,64,8192]{2,0,1:T(2,128)(2,1)}) %all-gather.11.cloned.1.call-update) | async-done | bytes 1048592 | tf_op jit(solution)/shard_map/all_gather | solution.py:134
  56.3 3.2 fusion.27
  62.0 24.2 %all_gather.31 = bf16[64,4096]{1,0:T(8,128)(2,1)S(1)} all-gather(bf16[64,128]{1,0:T(8,128)(2,1)S(1)} %fusion.77), channel_id=1, replica_groups=mesh['pipe'=4,'head'=32] {'head'}, dimensions={1}, use_global_device_ids=true | all-gather | bytes 540672 | tf_op jit(solution)/shard_map/all_gather | solution.py:74
  88.9 3.1 copy.232
  92.0 3.0 fusion.283
  95.0 2.4 copy.336
  98.1 5.0 fusion.13
  105.5 2.4 copy.335
  113.8 6.0 convolution_convert_fusion.4
  121.3 101.3 %all-reduce.6.cloned.1.call-done = bf16[64,8192]{1,0:T(8,128)(2,1)} async-done(((bf16[64,8192]{1,0:T(8,128)(2,1)}), bf16[64,8192]{1,0:T(8,128)(2,1)}) %all-reduce.6.cloned.1.call-update) | async-done | bytes 1048592 | tf_op jit(solution)/shard_map/psum | solution.py:152
  222.7 2.4 fusion.30
  227.4 2.8 fusion.46
  230.1 39.6 %all-gather.13.cloned.1.call-done = bf16[1,64,8192]{2,0,1:T(2,128)(2,1)} async-done(((bf16[1,2,8192]{2,0,1:T(2,128)(2,1)}), bf16[1,64,8192]{2,0,1:T(2,128)(2,1)}) %all-gather.13.cloned.1.call-update) | async-done | bytes 1048592 | tf_op jit(solution)/shard_map/all_gather | solution.py:134
  269.7 3.5 fusion.15
  275.3 5.0 fusion.11
  281.7 24.1 %all_gather.33 = bf16[64,4096]{1,0:T(8,128)(2,1)S(1)} all-gather(bf16[64,128]{1,0:T(8,128)(2,1)S(1)} %fusion.80), channel_id=1, replica_groups=mesh['pipe'=4,'head'=32] {'head'}, dimensions={1}, use_global_device_ids=true | all-gather | bytes 540672 | tf_op jit(solution)/shard_map/all_gather | solution.py:74
  309.2 3.1 copy.247
  312.4 3.0 fusion.282
  315.4 2.4 copy.339
  317.8 2.3 convolution_bitcast_fusion.6
  323.9 2.4 copy.338
  327.8 2.1 fusion.60
  332.0 6.0 convolution_convert_fusion.3
  339.5 101.4 %all-reduce.8.cloned.1.call-done = bf16[64,8192]{1,0:T(8,128)(2,1)} async-done(((bf16[64,8192]{1,0:T(8,128)(2,1)}), bf16[64,8192]{1,0:T(8,128)(2,1)}) %all-reduce.8.cloned.1.call-update) | async-done | bytes 1048592 | tf_op jit(solution)/shard_map/psum | solution.py:152
  440.9 2.6 fusion.18
  447.6 39.5 %all-gather.15.cloned.1.call-done = bf16[1,64,8192]{2,0,1:T(2,128)(2,1)} async-done(((bf16[1,2,8192]{2,0,1:T(2,128)(2,1)}), bf16[1,64,8192]{2,0,1:T(2,128)(2,1)}) %all-gather.15.cloned.1.call-update) | async-done | bytes 1048592 | tf_op jit(solution)/shard_map/all_gather | solution.py:134
  487.0 3.5 fusion.19
  492.6 5.0 fusion.9
  498.4 24.1 %all_gather.35 = bf16[64,4096]{1,0:T(8,128)(2,1)S(1)} all-gather(bf16[64,128]{1,0:T(8,128)(2,1)S(1)} %fusion.83), channel_id=1, replica_groups=mesh['pipe'=4,'head'=32] {'head'}, dimensions={1}, use_global_device_ids=true | all-gather | bytes 540672 | tf_op jit(solution)/shard_map/all_gather | solution.py:74
  525.3 3.1 copy.264
  528.4 3.1 fusion.281
  531.5 2.4 copy.342
  533.9 2.2 convolution_bitcast_fusion.4
  538.7 2.4 copy.341
  542.6 2.1 fusion.62
  546.8 6.0 convolution_convert_fusion.2
  554.3 101.4 %all-reduce.10.cloned.1.call-done = bf16[64,8192]{1,0:T(8,128)(2,1)} async-done(((bf16[64,8192]{1,0:T(8,128)(2,1)}), bf16[64,8192]{1,0:T(8,128)(2,1)}) %all-reduce.10.cloned.1.call-update) | async-done | bytes 1048592 | tf_op jit(solution)/shard_map/psum | solution.py:152
  655.7 2.4 fusion.22
  660.4 2.7 fusion.44
  663.1 39.1 %all-gather.17.cloned.1.call-done = bf16[1,64,8192]{2,0,1:T(2,128)(2,1)} async-done(((bf16[1,2,8192]{2,0,1:T(2,128)(2,1)}), bf16[1,64,8192]{2,0,1:T(2,128)(2,1)}) %all-gather.17.cloned.1.call-update) | async-done | bytes 1048592 | tf_op jit(solution)/shard_map/all_gather | solution.py:134
  702.2 3.5 fusion.23
  707.7 5.0 fusion.7
  714.2 24.1 %all_gather.37 = bf16[64,4096]{1,0:T(8,128)(2,1)S(1)} all-gather(bf16[64,128]{1,0:T(8,128)(2,1)S(1)} %fusion.86), channel_id=1, replica_groups=mesh['pipe'=4,'head'=32] {'head'}, dimensions={1}, use_global_device_ids=true | all-gather | bytes 540672 | tf_op jit(solution)/shard_map/all_gather | solution.py:74
  741.6 3.1 copy.281
  744.8 3.1 fusion.280
  747.9 2.4 copy.345
  750.3 2.2 convolution_bitcast_fusion.2
  755.7 2.4 copy.344
  759.7 2.1 fusion.64
  763.1 6.1 convolution_convert_fusion.1
  776.1 2.7 fusion.43
  778.8 93.3 %all-reduce.12.cloned.1.call-done = bf16[64,8192]{1,0:T(8,128)(2,1)} async-done(((bf16[64,8192]{1,0:T(8,128)(2,1)}), bf16[64,8192]{1,0:T(8,128)(2,1)}) %all-reduce.12.cloned.1.call-update) | async-done | bytes 1048592 | tf_op jit(solution)/shard_map/psum | solution.py:152
  872.2 2.4 fusion.26
  877.5 40.9 %all-gather.19.cloned.1.call-done = bf16[1,64,8192]{2,0,1:T(2,128)(2,1)} async-done(((bf16[1,2,8192]{2,0,1:T(2,128)(2,1)}), bf16[1,64,8192]{2,0,1:T(2,128)(2,1)}) %all-gather.19.cloned.1.call-update) | async-done | bytes 1048592 | tf_op jit(solution)/shard_map/all_gather | solution.py:134
  918.4 3.2 multiply_reduce_fusion
  924.0 4.9 fusion.5
  930.3 24.1 %all_gather.39 = bf16[64,4096]{1,0:T(8,128)(2,1)S(1)} all-gather(bf16[64,128]{1,0:T(8,128)(2,1)S(1)} %fusion.89), channel_id=1, replica_groups=mesh['pipe'=4,'head'=32] {'head'}, dimensions={1}, use_global_device_ids=true | all-gather | bytes 540672 | tf_op jit(solution)/shard_map/all_gather | solution.py:74
  955.2 2.0 copy.298
  957.2 2.7 fusion.279
  961.1 2.3 convolution_bitcast_fusion
  963.8 2.4 copy.347
  969.4 1.9 fusion.67
  971.8 6.0 convolution_convert_fusion
  979.4 101.3 %all-reduce.14.cloned.1.call-done = bf16[64,8192]{1,0:T(8,128)(2,1)} async-done(((bf16[64,8192]{1,0:T(8,128)(2,1)}), bf16[64,8192]{1,0:T(8,128)(2,1)}) %all-reduce.14.cloned.1.call-update) | async-done | bytes 1048592 | tf_op jit(solution)/shard_map/psum | solution.py:152
  (310 shorter events, 94.5 us)
Async XLA Ops:
  7.2 54.4 %copy-start = (bf16[1,8192,128]{2,1,0:T(8,128)(2,1)S(1)}, bf16[1,8192,128]{2,1,0:T(8,128)(2,1)}, u32[]{:S(2)}) copy-start(bf16[1,8192,128]{2,1,0:T(8,128)(2,1)} %param.17) | copy-start | bytes 6291460
  7.2 52.4 %copy-start.14 = (f32[1,8192]{1,0:T(1,128)S(1)}, f32[1,8192]{1,0:T(1,128)}, u32[]{:S(2)}) copy-start(f32[1,8192]{1,0:T(1,128)} %param.15) | copy-start | bytes 98308
  7.2 52.4 %copy-start.69 = (f32[1,8]{1,0:T(1,128)S(1)}, f32[1,8]{1,0:T(1,128)}, u32[]{:S(2)}) copy-start(f32[1,8]{1,0:T(1,128)} %param.22) | copy-start | bytes 100
  7.2 52.4 %copy-start.74 = (f32[1,8]{1,0:T(1,128)S(1)}, f32[1,8]{1,0:T(1,128)}, u32[]{:S(2)}) copy-start(f32[1,8]{1,0:T(1,128)} %param.21) | copy-start | bytes 100
  7.2 52.4 %copy-start.31 = (bf16[1,8192,8]{1,2,0:T(8,128)(2,1)S(1)}, bf16[1,8192,8]{1,2,0:T(8,128)(2,1)}, u32[]{:S(2)}) copy-start(bf16[1,8192,8]{1,2,0:T(8,128)(2,1)} %param.18) | copy-start | bytes 393220
  7.2 49.1 %all-gather.11.cloned.1.call-start = ((), (), s32[]{:S(2)}) async-start(), calls=%async_computation.5 | async-start | bytes 2162688 | tf_op jit(solution)/shard_map/all_gather | solution.py:134
  9.7 212.9 %all-reduce.6.cloned.1.call-start = ((), (), s32[]{:S(2)}) async-start(), calls=%async_computation | async-start | bytes 2097152 | tf_op jit(solution)/shard_map/psum | solution.py:152
  11.8 749.9 %copy-start.23 = (pred[64,64]{0,1:T(8,128)(4,1)}, pred[64,64]{0,1:T(8,128)(4,1)S(1)}, u32[]{:S(2)}) copy-start(pred[64,64]{0,1:T(8,128)(4,1)S(1)} %iota_compare_fusion) | copy-start | bytes 12292
  12.7 90.4 %copy-start.40 = (f32[1,1,512]{2,1,0:T(1,128)}, f32[1,1,512]{2,1,0:T(1,128)S(1)}, u32[]{:S(2)}) copy-start(f32[1,1,512]{2,1,0:T(1,128)S(1)} %get-tuple-element.41) | copy-start | bytes 6148
  12.7 90.4 %copy-start.45 = (f32[1,1,512]{2,1,0:T(1,128)}, f32[1,1,512]{2,1,0:T(1,128)S(1)}, u32[]{:S(2)}) copy-start(f32[1,1,512]{2,1,0:T(1,128)S(1)} %get-tuple-element.42) | copy-start | bytes 6148
  12.7 741.2 %copy-start.36 = (f32[1,1,512]{2,1,0:T(1,128)}, f32[1,1,512]{2,1,0:T(1,128)S(1)}, u32[]{:S(2)}) copy-start(f32[1,1,512]{2,1,0:T(1,128)S(1)} %get-tuple-element.39) | copy-start | bytes 6148
  12.7 741.2 %copy-start.38 = (f32[1,1,512]{2,1,0:T(1,128)}, f32[1,1,512]{2,1,0:T(1,128)S(1)}, u32[]{:S(2)}) copy-start(f32[1,1,512]{2,1,0:T(1,128)S(1)} %get-tuple-element.40) | copy-start | bytes 6148
  13.8 726.2 %copy-start.16 = (f32[1,1,4096]{2,1,0:T(1,128)}, f32[1,1,4096]{2,1,0:T(1,128)S(1)}, u32[]{:S(2)}) copy-start(f32[1,1,4096]{2,1,0:T(1,128)S(1)} %get-tuple-element.38) | copy-start | bytes 49156
  107.9 4.6 copy-start.53
  107.9 4.6 copy-start.63
  109.4 4.0 copy-start.64
  119.8 150.0 %all-gather.13.cloned.1.call-start = ((), (), s32[]{:S(2)}) async-start(), calls=%async_computation.6 | async-start | bytes 2162688 | tf_op jit(solution)/shard_map/all_gather | solution.py:134
  121.3 319.6 %all-reduce.8.cloned.1.call-start = ((), (), s32[]{:S(2)}) async-start(), calls=%async_computation.1 | async-start | bytes 2097152 | tf_op jit(solution)/shard_map/psum | solution.py:152
  225.1 44.7 %collective-permute-start = (bf16[64,8192]{1,0:T(8,128)(2,1)}, bf16[64,8192]{1,0:T(8,128)(2,1)}, u32[]{:S(2)}, u32[]{:S(2)}) collective-permute-start(bf16[64,8192]{1,0:T(8,128)(2,1)} %fusion.30), channel_id=1, source_target_pairs={{0,32},{32,64},{64,96},{1,33},{33,65},{65,97},{2,34},{34,66},{66,9... | collective-permute-start | bytes 3145736 | tf_op jit(solution)/shard_map/ppermute | solution.py:14
  280.3 25.7 %copy-start.26 = (f32[1,3,4096]{2,0,1:T(1,128)S(1)}, f32[1,3,4096]{2,0,1:T(1,128)}, u32[]{:S(2)}) copy-start(f32[1,3,4096]{2,0,1:T(1,128)} %param.27) | copy-start | bytes 147460
  312.4 5.4 copy-start.55
  315.4 4.7 copy-start.30
  315.4 5.3 copy-start.61
  315.4 6.7 copy-start.41
  315.4 6.7 copy-start.46
  326.2 5.3 copy-start.65
  338.0 149.0 %all-gather.15.cloned.1.call-start = ((), (), s32[]{:S(2)}) async-start(), calls=%async_computation.7 | async-start | bytes 2162688 | tf_op jit(solution)/shard_map/all_gather | solution.py:134
  339.5 316.2 %all-reduce.10.cloned.1.call-start = ((), (), s32[]{:S(2)}) async-start(), calls=%async_computation.2 | async-start | bytes 2097152 | tf_op jit(solution)/shard_map/psum | solution.py:152
  440.9 5.0 copy-start.3
  440.9 5.0 copy-start.8
  443.5 43.5 %collective-permute-start.1 = (bf16[64,8192]{1,0:T(8,128)(2,1)}, bf16[64,8192]{1,0:T(8,128)(2,1)}, u32[]{:S(2)}, u32[]{:S(2)}) collective-permute-start(bf16[64,8192]{1,0:T(8,128)(2,1)} %fusion.18), channel_id=1, source_target_pairs={{0,32},{32,64},{64,96},{1,33},{33,65},{65,97},{2,34},{34,66},{66,9... | collective-permute-start | bytes 3145736 | tf_op jit(solution)/shard_map/ppermute | solution.py:14
  497.6 39.3 %copy-start.20 = (f32[64,512]{1,0:T(8,128)}, f32[64,512]{1,0:T(8,128)S(1)}, u32[]{:S(2)}) copy-start(f32[64,512]{1,0:T(8,128)S(1)} %fusion.9) | copy-start | bytes 393220
  497.6 26.1 %copy-start.18 = (f32[3,4096]{1,0:T(4,128)S(1)}, f32[3,4096]{1,0:T(4,128)}, u32[]{:S(2)}) copy-start(f32[3,4096]{1,0:T(4,128)} %get-tuple-element.12) | copy-start | bytes 147460
  528.4 5.5 copy-start.56
  531.5 5.3 copy-start.42
  531.5 5.3 copy-start.47
  531.5 5.3 copy-start.50
  541.0 5.3 copy-start.66
  552.8 149.4 %all-gather.17.cloned.1.call-start = ((), (), s32[]{:S(2)}) async-start(), calls=%async_computation.8 | async-start | bytes 2162688 | tf_op jit(solution)/shard_map/all_gather | solution.py:134
  554.3 317.9 %all-reduce.12.cloned.1.call-start = ((), (), s32[]{:S(2)}) async-start(), calls=%async_computation.3 | async-start | bytes 2097152 | tf_op jit(solution)/shard_map/psum | solution.py:152
  658.1 44.1 %collective-permute-start.2 = (bf16[64,8192]{1,0:T(8,128)(2,1)}, bf16[64,8192]{1,0:T(8,128)(2,1)}, u32[]{:S(2)}, u32[]{:S(2)}) collective-permute-start(bf16[64,8192]{1,0:T(8,128)(2,1)} %fusion.22), channel_id=1, source_target_pairs={{0,32},{32,64},{64,96},{1,33},{33,65},{65,97},{2,34},{34,66},{66,9... | collective-permute-start | bytes 3145736 | tf_op jit(solution)/shard_map/ppermute | solution.py:14
  712.7 25.7 %copy-start.19 = (f32[3,4096]{1,0:T(4,128)S(1)}, f32[3,4096]{1,0:T(4,128)}, u32[]{:S(2)}) copy-start(f32[3,4096]{1,0:T(4,128)} %get-tuple-element.12) | copy-start | bytes 147460
  712.9 28.7 %copy-start.22 = (f32[64,8]{1,0:T(8,128)}, f32[64,8]{1,0:T(8,128)S(1)}, u32[]{:S(2)}) copy-start(f32[64,8]{1,0:T(8,128)S(1)} %reduce_window_sum.30) | copy-start | bytes 6148
  744.8 5.5 copy-start.57
  747.9 4.7 copy-start.29
  747.9 4.7 copy-start.51
  747.9 6.1 copy-start.43
  747.9 6.1 copy-start.48
  754.7 7.1 copy-start.52
  754.7 7.1 copy-start.62
  758.1 4.6 copy-start.67
  763.1 6.2 copy-start.27
  769.2 149.2 %all-gather.19.cloned.1.call-start = ((), (), s32[]{:S(2)}) async-start(), calls=%async_computation.9 | async-start | bytes 2162688 | tf_op jit(solution)/shard_map/all_gather | solution.py:134
  770.0 310.7 %all-reduce.14.cloned.1.call-start = ((), (), s32[]{:S(2)}) async-start(), calls=%async_computation.4 | async-start | bytes 2097152 | tf_op jit(solution)/shard_map/psum | solution.py:152
  778.8 97.0 %copy-start.28 = (bf16[1,2,8192]{2,1,0:T(2,128)(2,1)S(1)}, bf16[1,2,8192]{2,1,0:T(2,128)(2,1)}, u32[]{:S(2)}) copy-start(bf16[1,2,8192]{2,1,0:T(2,128)(2,1)} %constant_dynamic-slice_fusion) | copy-start | bytes 98308
  874.6 43.8 %collective-permute-start.3 = (bf16[64,8192]{1,0:T(8,128)(2,1)}, bf16[64,8192]{1,0:T(8,128)(2,1)S(1)}, u32[]{:S(2)}, u32[]{:S(2)}) collective-permute-start(bf16[64,8192]{1,0:T(8,128)(2,1)} %fusion.26), channel_id=1, source_target_pairs={{0,32},{32,64},{64,96},{1,33},{33,65},{65,97},{2,34},{34,66},{66,9... | collective-permute-start | bytes 3145736 | tf_op jit(solution)/shard_map/ppermute | solution.py:14
  928.9 25.6 %copy-start.17 = (f32[1,1,4096]{2,1,0:T(1,128)S(1)}, f32[1,1,4096]{2,1,0:T(1,128)}, u32[]{:S(2)}) copy-start(f32[1,1,4096]{2,1,0:T(1,128)} %copy-done.16) | copy-start | bytes 49156
  928.9 25.6 %copy-start.25 = (f32[3,4096]{1,0:T(4,128)S(1)}, f32[3,4096]{1,0:T(4,128)}, u32[]{:S(2)}) copy-start(f32[3,4096]{1,0:T(4,128)} %get-tuple-element.4) | copy-start | bytes 147460
  961.1 6.5 copy-start.2
  963.6 5.8 copy-start.24
  963.6 5.8 copy-start.54
  963.6 5.8 copy-start.59
  966.1 5.2 copy-start.68
  971.8 6.1 copy-start.79
  (30 other events, 59.1 us)
Sparse Core Ops, SparseCore 0:
  10.9 45.4 all-gather.10
  119.9 102.7 all-reduce.5
  225.8 43.9 all-gather.12
  338.1 102.7 all-reduce.7
  443.0 43.9 all-gather.14
  552.9 102.7 all-reduce.9
  658.2 43.9 all-gather.16
  769.4 102.7 all-reduce.11
  874.4 43.9 all-gather.18
  977.9 102.7 all-reduce.13
where the time goes:
time: 1100 us; the launch traced here: 1090 us
  waiting for transfers between devices  700 us (64%)
  blocking collectives  121 us (11%)
  matrix products  111 us (10%)
  local copies, waits for them, and re-layouts  82 us (7%)
  other arithmetic  53.4 us (5%)
  between operations  15.9 us (1%)
    psum x5, waiting for transfers between devices, per_device(): lax.psum(jnp.dot(mixed_bf, out_weight, preferred_element_type=jnp.float32...  499 us
    all_gather x5, waiting for transfers between devices, per_device(): entry_rows = lax.all_gather(own_rows, 'head', axis=0, tiled=True)  202 us
    all_gather x5, blocking collectives, mix_block(): bc_all = lax.all_gather(bc_part, 'head', axis=1, tiled=True)  121 us
    unnamed x178, local copies, waits for them, and re-layouts  35 us
    dot_general x5, matrix products, per_device(): jnp.dot(mixed_bf, out_weight, preferred_element_type=jnp.float32)  30 us
    dot_general x5, matrix products, mix_block(): x_proj = jnp.dot(normed, proj_x, preferred_element_type=jnp.float32)  24.9 us
  transfers between devices with their start and end apart: 14, of which 10 were waited for; matrix products, arithmetic and copies ran while one was open for 4% of the time, Pallas kernels for 0%

commit v1 on v0

v1 whole, which is shorter than its diff:
```python
import functools

import jax
import jax.numpy as jnp
from jax import lax
from jax.experimental import pallas as pl
from jax.experimental.pallas import tpu as pltpu
from jax.sharding import PartitionSpec as P

GROUPS = 8
STATE = 256
HEAD_DIM = 64
MESH = pl.DeviceIdType.MESH
F32 = jnp.float32
BF16 = jnp.bfloat16
AHEAD = 3


def dot(a, b, dims=((1,), (0,)), precision=None):
    return lax.dot_general(a, b, (dims, ((), ())), precision=precision, preferred_element_type=F32)


def exact(a, b):
    return dot(a, b, precision=lax.Precision.HIGHEST)


def section(
    sizes,
    hid,
    gain,
    w_x,
    w_bc,
    w_dt,
    w_out,
    ssm_in,
    taps,
    tails,
    dt_bias,
    a_rate,
    d_skip,
    out,
    state,
    wx_v,
    wbd_v,
    wdt_v,
    wo_v,
    ssm_v,
    ssm_t,
    h_all,
    first_in,
    acc,
    squares,
    padded,
    bc_send,
    bc_recv,
    y_v,
    x_end,
    b_end,
    decay_end,
    sib_send,
    sib_recv,
    sum_send,
    sum_recv,
    total,
    passed,
    out_send,
    load_sem,
    first_s,
    first_r,
    ag_s,
    ag_r,
    fwd_r,
    bc_s,
    bc_r,
    sib_s,
    sib_r,
    sum_s,
    sum_r,
    pass_s,
    pass_r,
    out_s,
    out_r,
    own_s,
):
    n_pipe, n_head, n_x, n_y = sizes
    n_chip = n_head // 2
    micro = hid.shape[0]
    rows = hid.shape[1]
    width = hid.shape[2]
    tokens = rows * n_head
    chunk = width // n_head
    inner = w_x.shape[2]
    heads = dt_bias.shape[1]
    bc_cols = w_bc.shape[2]
    per_group = n_head // GROUPS
    z = lax.axis_index("pipe")
    me = lax.axis_index("head")
    core = lax.rem(me, 2)
    chip = lax.div(me, 2)
    chip_x = lax.rem(chip, n_x)
    chip_y = lax.div(chip, n_x)
    sibling = chip * 2 + 1 - core

    def ahead(t):
        return lax.rem(chip_y + lax.div(t, n_x), n_y) * n_x + lax.rem(chip_x + lax.rem(t, n_x), n_x)

    def behind(t):
        return lax.rem(chip_y + n_y - lax.div(t, n_x), n_y) * n_x + lax.rem(
            chip_x + n_x - lax.rem(t, n_x), n_x
        )

    def remote(src, dst, send, recv, head, pipe=None):
        return pltpu.make_async_remote_copy(
            src_ref=src,
            dst_ref=dst,
            send_sem=send,
            recv_sem=recv,
            device_id={"pipe": z if pipe is None else pipe, "head": head},
            device_id_type=MESH,
        )

    def drain(ref, sem):
        pltpu.make_async_copy(ref, ref, sem).wait()

    def each(first, last, body):
        def step(t, carry):
            body(t)
            return carry

        lax.fori_loop(first, last, step, 0)

    def load_in(k):
        pltpu.make_async_copy(w_x.at[k], wx_v.at[k], load_sem.at[0]).start()
        pltpu.make_async_copy(w_bc.at[k], wbd_v.at[k, :, pl.ds(0, bc_cols)], load_sem.at[1]).start()

    each(0, n_chip, load_in)
    pltpu.make_async_copy(w_dt, wdt_v, load_sem.at[2]).start()
    pltpu.make_async_copy(ssm_in, ssm_v, load_sem.at[3]).start()
    for k in range(n_head):
        pltpu.make_async_copy(
            w_out.at[:, pl.ds(k * chunk, chunk)], wo_v.at[k], load_sem.at[4]
        ).start()

    barrier = pltpu.get_barrier_semaphore()

    def greet(t):
        pl.semaphore_signal(
            barrier,
            inc=1,
            device_id={"pipe": z, "head": lax.rem(me + t, n_head)},
            device_id_type=MESH,
        )

    each(1, n_head, greet)
    for other in (lax.rem(z + 1, n_pipe), lax.rem(z + n_pipe - 1, n_pipe)):
        pl.semaphore_signal(
            barrier, inc=1, device_id={"pipe": other, "head": me}, device_id_type=MESH
        )
    pl.semaphore_wait(barrier, n_head + 1)

    @pl.when(z == 0)
    def _():
        for m in range(micro):

            def give(t):
                to = lax.rem(me + t, n_head)
                remote(
                    hid.at[m, :, pl.ds(pl.multiple_of(to * chunk, chunk), chunk)],
                    first_in.at[m, me],
                    first_s.at[m],
                    first_r.at[m],
                    to,
                ).start()

            each(1, n_head, give)
            pltpu.make_async_copy(
                hid.at[m, :, pl.ds(pl.multiple_of(me * chunk, chunk), chunk)],
                first_in.at[m, me],
                own_s,
            ).start()
            drain(first_in.at[m, 0], own_s)

    def spread(m):
        mine = h_all.at[m, me]

        def give(t):
            remote(mine, mine, ag_s, ag_r.at[m, t], ahead(t) * 2 + core).start()

        each(1, n_chip, give)
        remote(mine, mine, ag_s, fwd_r.at[m, 0], sibling).start()

    def begin(m):
        drain(first_in.at[m, pl.ds(0, n_head - 1)], first_r.at[m])
        for i in range(n_head):
            total[pl.ds(i * rows, rows), :] = first_in[m, i].astype(F32)
        h_all[m, me] = total[...].astype(BF16)
        spread(m)

    @pl.when(z == 0)
    def _():
        begin(0)

    drain(wdt_v, load_sem.at[2])
    for_pad = jnp.zeros((2 * chunk, 256 - bc_cols - heads), BF16)

    def join(k):
        wbd_v[k, :, bc_cols:256] = jnp.concatenate([wdt_v[k], for_pad], axis=1)

    each(0, n_chip, join)
    drain(ssm_v, load_sem.at[3])
    ssm_t[...] = ssm_v[...].reshape(heads * HEAD_DIM, STATE).T
    padded[5:8, :] = tails[...]
    drain(wx_v, load_sem.at[0])
    drain(wbd_v.at[:, :, pl.ds(0, bc_cols)], load_sem.at[1])

    def block(m):
        @pl.when(jnp.logical_and(z == 0, m > 0))
        def _():
            begin(m)

        @pl.when(z > 0)
        def _():
            remote(passed.at[m], h_all.at[m, me], pass_s, pass_r.at[m], me).wait_recv()
            spread(m)

        acc[...] = jnp.zeros_like(acc)
        squares[...] = jnp.zeros_like(squares)

        def relay(t):
            got = h_all.at[m, behind(t) * 2 + core]
            copy = remote(got, got, ag_s, ag_r.at[m, t], sibling)
            copy.wait_recv()
            remote(got, got, ag_s, fwd_r.at[m, t], sibling).start()

        each(1, 1 + AHEAD, relay)

        def project(t):
            @pl.when(t + 1 + AHEAD < n_chip)
            def _():
                relay(t + 1 + AHEAD)

            src = behind(t)
            theirs = h_all.at[m, src * 2 + 1 - core]
            remote(theirs, theirs, ag_s, fwd_r.at[m, t], sibling).wait_recv()
            values = jnp.concatenate([h_all[m, src * 2], h_all[m, src * 2 + 1]], axis=1).astype(F32)
            sq = values * values
            part = sq[:, 0:128]
            for k in range(1, 2 * chunk // 128):
                part = part + sq[:, k * 128 : (k + 1) * 128]
            squares[...] += part
            scaled = (values * gain[src]).astype(BF16)
            acc[:, 0:inner] += dot(scaled, wx_v[src])
            acc[:, inner : inner + 256] += dot(scaled, wbd_v[src])

        each(0, n_chip, project)
        inv = lax.rsqrt(jnp.sum(squares[...], axis=1, keepdims=True) / width + 1e-05)

        bc_dt = acc[:, inner : inner + 256] * inv
        bc_bf = bc_dt[:, 0:bc_cols].astype(BF16)
        bc_wide = jnp.concatenate([bc_bf, jnp.zeros((128 - tokens, bc_cols), BF16)], axis=0)
        at_row = lax.broadcasted_iota(jnp.int32, (bc_cols, bc_cols), 0)
        at_col = lax.broadcasted_iota(jnp.int32, (bc_cols, bc_cols), 1)
        width_n = bc_cols // GROUPS
        wanted = lax.rem(at_row, width_n) * GROUPS + lax.div(at_row, width_n)
        order = jnp.where(at_col == wanted, 1.0, 0.0).astype(BF16)
        bc_send[...] = dot(order, bc_wide, ((1,), (1,))).astype(BF16).reshape(bc_send.shape)

        def give_bc(t):
            to = lax.rem(me + t, n_head)
            remote(
                bc_send.at[lax.div(to, per_group)], bc_recv.at[m, me], bc_s, bc_r.at[m], to
            ).start()

        each(1, n_head, give_bc)
        bc_recv[m, me] = bc_send[lax.div(me, per_group)]

        padded[8 : 8 + tokens, 0:inner] = acc[:, 0:inner] * inv

        def conv(lo, hi):
            summed = taps[0:1, lo:hi] * padded[5 : 5 + tokens, lo:hi]
            for k in range(1, 4):
                summed = summed + taps[k : k + 1, lo:hi] * padded[5 + k : 5 + k + tokens, lo:hi]
            return summed * lax.logistic(summed)

        x = conv(0, inner)
        raw = bc_dt[:, bc_cols : bc_cols + heads] + dt_bias[...]
        step = jnp.maximum(raw, 0.0) + jnp.log1p(jnp.exp(-jnp.abs(raw)))
        tri_row = lax.broadcasted_iota(jnp.int32, (tokens, tokens), 0)
        tri_col = lax.broadcasted_iota(jnp.int32, (tokens, tokens), 1)
        log_decay = exact(jnp.where(tri_row >= tri_col, 1.0, 0.0), -step * a_rate[...])
        head_row = lax.broadcasted_iota(jnp.int32, (heads, inner), 0)
        head_col = lax.div(lax.broadcasted_iota(jnp.int32, (heads, inner), 1), HEAD_DIM)
        of_head = jnp.where(head_row == head_col, 1.0, 0.0)
        skip8 = jnp.broadcast_to(d_skip[...], (8, heads))
        wide = exact(jnp.concatenate([step, log_decay, skip8], axis=0), of_head)
        step_w = wide[0:tokens]
        log_w = wide[tokens : 2 * tokens]
        skip_w = wide[2 * tokens : 2 * tokens + 1]
        at_t = lax.broadcasted_iota(jnp.int32, (tokens, inner), 0)
        at_s = lax.rem(lax.broadcasted_iota(jnp.int32, (tokens, inner), 1), HEAD_DIM)
        log_s = jnp.sum(jnp.where(at_t == at_s, log_w, 0.0), axis=0, keepdims=True)
        causal = at_t >= at_s
        pair = jnp.where(causal, jnp.exp(jnp.where(causal, log_w - log_s, 0.0)), 0.0)
        log_end = log_w[tokens - 1 : tokens]
        x_dt = x * step_w
        x_end[...] = (jnp.exp(log_end - log_w) * x_dt).astype(BF16)
        decay_end[0:1, :] = jnp.exp(log_end)

        drain(bc_recv.at[m, pl.ds(0, n_head - 1)], bc_r.at[m])
        both = bc_recv[m].reshape(2 * STATE, 128).astype(F32).T
        padded[8 : 8 + tokens, inner : inner + 2 * STATE] = both[0:tokens]
        bc = conv(inner, inner + 2 * STATE)
        padded[5:8, :] = padded[5 + tokens : 8 + tokens, :]
        b_v = bc[:, 0:STATE].astype(BF16)
        c_v = bc[:, STATE : 2 * STATE].astype(BF16)
        b_end[...] = b_v
        scores = dot(c_v, jnp.concatenate([b_v, b_v], axis=0), ((1,), (1,)))
        weight = (jnp.concatenate([scores] * (heads // 2), axis=1) * pair).astype(BF16)
        lane = lax.broadcasted_iota(jnp.int32, (tokens, 2 * HEAD_DIM), 1)
        within = []
        for k in range(heads // 2):
            cols = slice(k * 2 * HEAD_DIM, (k + 1) * 2 * HEAD_DIM)
            two = x_dt[:, cols]
            stacked = jnp.concatenate(
                [jnp.where(lane < HEAD_DIM, two, 0.0), jnp.where(lane < HEAD_DIM, 0.0, two)], axis=0
            ).astype(BF16)
            within.append(dot(weight[:, cols], stacked))
        carried = jnp.exp(log_w) * dot(c_v, ssm_t[...].astype(BF16))
        y_v[...] = (jnp.concatenate(within, axis=1) + carried + skip_w * x).astype(BF16)

        @pl.when(m == 0)
        def _():
            drain(wo_v, load_sem.at[4])

        def for_sibling(i):
            t = lax.rem(i + 1, n_chip)
            sib_send[t] = dot(y_v[...], wo_v[ahead(t) * 2 + 1 - core]).astype(BF16)
            remote(sib_send.at[t], sib_recv.at[m, t], sib_s, sib_r.at[m, t], sibling).start()

        each(0, n_chip, for_sibling)

        def chip_sum(t):
            part = dot(y_v[...], wo_v[ahead(t) * 2 + core]).astype(BF16).astype(F32)
            remote(
                sib_send.at[t], sib_recv.at[m, t], sib_s, sib_r.at[m, t], sibling
            ).wait_recv()
            return part + sib_recv[m, t].astype(F32)

        def for_owner(t):
            sum_send[t] = chip_sum(t).astype(BF16)
            remote(
                sum_send.at[t],
                sum_recv.at[m, t],
                sum_s,
                sum_r.at[m, t],
                ahead(t) * 2 + core,
            ).start()

        each(1, n_chip, for_owner)
        total[...] = chip_sum(0) + h_all[m, me].astype(F32)

        ssm_t[...] = decay_end[0:1, :] * ssm_t[...] + dot(b_end[...], x_end[...], ((0,), (0,)))

        @pl.when(m == micro - 1)
        def _():
            state[...] = ssm_t[...].T.reshape(state.shape)

        def take(t):
            remote(
                sum_send.at[t], sum_recv.at[m, t], sum_s, sum_r.at[m, t], sibling
            ).wait_recv()
            total[...] += sum_recv[m, t].astype(F32)

        each(1, n_chip, take)
        passed[m] = total[...].astype(BF16)

        @pl.when(z < n_pipe - 1)
        def _():
            remote(passed.at[m], h_all.at[m, me], pass_s, pass_r.at[m], me, z + 1).start()

        for i in range(n_head):
            out_send[m, i] = total[pl.ds(i * rows, rows), :].astype(BF16)

        def give_out(t):
            to = lax.rem(me + t, n_head)
            remote(
                out_send.at[m, to],
                out.at[m, :, pl.ds(pl.multiple_of(me * chunk, chunk), chunk)],
                out_s,
                out_r.at[m],
                to,
            ).start()

        each(1, n_head, give_out)
        pltpu.make_async_copy(
            out_send.at[m, me],
            out.at[m, :, pl.ds(pl.multiple_of(me * chunk, chunk), chunk)],
            own_s,
        ).start()

        drain(out_send.at[m, 0], own_s)
        drain(h_all.at[m, pl.ds(0, n_head - 1)], ag_s)
        drain(bc_recv.at[m, pl.ds(0, n_head - 1)], bc_s)
        drain(sib_send, sib_s)
        drain(sum_send.at[pl.ds(1, n_chip - 1)], sum_s)
        drain(out_send.at[m, pl.ds(0, n_head - 1)], out_s)

        @pl.when(z < n_pipe - 1)
        def _():
            remote(passed.at[m], h_all.at[m, me], pass_s, pass_r.at[m], me).wait_send()

        @pl.when(z == 0)
        def _():
            drain(first_in.at[m, pl.ds(0, n_head - 1)], first_s.at[m])

    each(0, micro, block)
    for m in range(micro):
        drain(out.at[m, :, pl.ds(0, (n_head - 1) * chunk)], out_r.at[m])


def per_device(
    sizes,
    hidden,
    norm_gain,
    w_x,
    w_bc,
    w_dt,
    conv_x,
    conv_bc,
    dt_bias,
    a_rate,
    d_skip,
    w_out,
    ssm_init,
    conv_x_init,
    conv_bc_init,
):
    n_pipe, n_head, n_x, n_y = sizes
    n_chip = n_head // 2
    micro, rows, width = hidden.shape
    tokens = rows * n_head
    chunk = width // n_head
    inner = w_x.shape[2]
    heads = dt_bias.shape[1]
    bc_cols = w_bc.shape[2]
    group = lax.axis_index("head") // (n_head // GROUPS)

    def own_group(values):
        split = values[0].reshape(values.shape[1], -1, GROUPS)
        return lax.dynamic_index_in_dim(split, group, 2, keepdims=False)

    taps = jnp.concatenate([conv_x[0], own_group(conv_bc)], axis=1)
    tails = jnp.concatenate([conv_x_init[0], own_group(conv_bc_init)], axis=1)
    vmem = pl.BlockSpec(memory_space=pltpu.VMEM)
    far = pl.BlockSpec(memory_space=pl.ANY)
    dma = pltpu.SemaphoreType.DMA
    out, state = pl.pallas_call(
        functools.partial(section, sizes),
        out_shape=(
            jax.ShapeDtypeStruct((micro, rows, width), BF16),
            jax.ShapeDtypeStruct(ssm_init.shape[1:], F32),
        ),
        in_specs=[vmem, vmem, far, far, far, far, far, vmem, vmem, vmem, vmem, vmem],
        out_specs=(vmem, vmem),
        scratch_shapes=[
            pltpu.VMEM((n_chip, 2 * chunk, inner), BF16),
            pltpu.VMEM((n_chip, 2 * chunk, 256), BF16),
            pltpu.VMEM((n_chip, 2 * chunk, heads), BF16),
            pltpu.VMEM((n_head, inner, chunk), BF16),
            pltpu.VMEM(ssm_init.shape[1:], F32),
            pltpu.VMEM((STATE, inner), F32),
            pltpu.VMEM((micro, n_head, tokens, chunk), BF16),
            pltpu.VMEM((micro, n_head, rows, chunk), BF16),
            pltpu.VMEM((tokens, inner + 256), F32),
            pltpu.VMEM((tokens, 128), F32),
            pltpu.VMEM((8 + tokens, inner + 2 * STATE), F32),
            pltpu.VMEM((GROUPS, bc_cols // GROUPS, 128), BF16),
            pltpu.VMEM((micro, n_head, bc_cols // GROUPS, 128), BF16),
            pltpu.VMEM((tokens, inner), BF16),
            pltpu.VMEM((tokens, inner), BF16),
            pltpu.VMEM((tokens, STATE), BF16),
            pltpu.VMEM((8, inner), F32),
            pltpu.VMEM((n_chip, tokens, chunk), BF16),
            pltpu.VMEM((micro, n_chip, tokens, chunk), BF16),
            pltpu.VMEM((n_chip, tokens, chunk), BF16),
            pltpu.VMEM((micro, n_chip, tokens, chunk), BF16),
            pltpu.VMEM((tokens, chunk), F32),
            pltpu.VMEM((micro, tokens, chunk), BF16),
            pltpu.VMEM((micro, n_head, rows, chunk), BF16),
            dma((5,)),
            dma((micro,)),
            dma((micro,)),
            dma,
            dma((micro, n_chip)),
            dma((micro, n_chip)),
            dma,
            dma((micro,)),
            dma,
            dma((micro, n_chip)),
            dma,
            dma((micro, n_chip)),
            dma,
            dma((micro,)),
            dma,
            dma((micro,)),
            dma,
        ],
        compiler_params=pltpu.CompilerParams(
            collective_id=0, has_side_effects=True, vmem_limit_bytes=48 << 20
        ),
    )(
        hidden,
        norm_gain.reshape(n_chip, 1, 2 * chunk),
        w_x.reshape(n_chip, 2 * chunk, inner),
        w_bc.reshape(n_chip, 2 * chunk, bc_cols),
        w_dt.reshape(n_chip, 2 * chunk, heads),
        w_out[0],
        ssm_init[0],
        taps,
        tails,
        dt_bias,
        a_rate,
        d_skip,
    )
    return (out[None], state[None])


def solution(mesh):
    n_pipe = mesh.shape["pipe"]
    n_head = mesh.shape["head"]
    n_x = 1
    while n_x * n_x < n_head // 2:
        n_x *= 2
    in_specs = (
        P(None, "head", None),
        P("pipe", None),
        P("pipe", None, "head"),
        P("pipe", None, "head"),
        P("pipe", None, "head"),
        P("pipe", None, "head"),
        P("pipe", None, None),
        P("pipe", "head"),
        P("pipe", "head"),
        P("pipe", "head"),
        P("pipe", "head", None),
        P("pipe", "head", None, None),
        P("pipe", None, "head"),
        P("pipe", None, None),
    )
    out_specs = (P("pipe", None, "head", None), P("pipe", "head", None, None))
    return jax.shard_map(
        functools.partial(per_device, (n_pipe, n_head, n_x, n_head // 2 // n_x)),
        mesh=mesh,
        in_specs=in_specs,
        out_specs=out_specs,
        check_vma=False,
    )
```

time: 1100 us -> 194 us (0.18)
  waiting for transfers between devices: 700 us -> 0 us
  Pallas kernels: 0 us -> 178 us
  blocking collectives: 121 us -> 0 us
  matrix products: 111 us -> 0 us
  local copies, waits for them, and re-layouts: 82 us -> 13.2 us
  other arithmetic: 53.4 us -> 1.64 us
  between operations: 15.9 us -> 0.71 us
    psum x5 -> x0, waiting for transfers between devices: 499 us -> none  [per_device(): lax.psum(jnp.dot(mixed_bf, out_weight, preferred_element_type=jnp.float32...]
    all_gather x5 -> x0, waiting for transfers between devices: 202 us -> none  [per_device(): entry_rows = lax.all_gather(own_rows, 'head', axis=0, tiled=True)]
    pallas_call x0 -> x1, Pallas kernels: none -> 178 us  [per_device(): pl.pallas_call(functools.partial(section, sizes), out_shape=(jax.ShapeDty...]
    all_gather x5 -> x0, blocking collectives: 121 us -> none  [mix_block(): bc_all = lax.all_gather(bc_part, 'head', axis=1, tiled=True)]
    dot_general x50 -> x0, matrix products: 111 us -> none  [the longest x5 30 us: per_device(): jnp.dot(mixed_bf, out_weight, preferred_element_type=jnp.float32)]
    unnamed x178 -> x18, local copies, waits for them, and re-layouts: 35 us -> 10.1 us
    reduce_sum x5 -> x0, other arithmetic: 17 us -> none  [rms_rows(): jnp.mean(floats * floats, axis=-1, keepdims=True) + 1e-05]
    slice x7 -> x0, local copies, waits for them, and re-layouts: 16.7 us -> none  [the longest x5 14.8 us: mix_block(): grouped[:, 0]]
  transfers between devices with their start and end apart: 14 -> 0, of which waited for: 10 -> 0; matrix products, arithmetic and copies ran while one was open for 4% -> 0% of each run, Pallas kernels for 0% -> 0%
where the time goes in v1:
time: 194 us; the launch traced here: 193 us
  Pallas kernels  178 us (92%)
  local copies, waits for them, and re-layouts  13.2 us (7%)
    pallas_call x1, Pallas kernels, per_device(): pl.pallas_call(functools.partial(section, sizes), out_shape=(jax.ShapeDty...  178 us
    unnamed x18, local copies, waits for them, and re-layouts  10.1 us

profile of v1, /device:TPU:97, one launch (start us, length us, event | category | flops | bytes accessed | tf_op | source)
XLA Modules:
  0.0 193.1 jit_solution(10743858842642290804)
XLA Ops:
  0.6 0.7 copy.23
  1.3 0.9 reduce.1
  2.3 0.4 reshape_squeeze.7
  2.7 0.5 dynamic-slice_reduce_fusion.1
  3.3 1.4 reshape_squeeze.6
  4.7 0.6 dynamic-slice_reduce_fusion
  5.3 0.7 pad_maximum_fusion.taps
  6.1 1.8 copy.20
  7.9 0.0 copy-start
  7.9 1.6 copy-done
  9.5 0.0 copy-start.1
  9.5 1.0 copy-done.1
  10.5 0.0 copy-start.2
  10.5 0.8 copy-done.2
  11.4 0.0 copy-start.3
  11.4 0.8 copy-done.3
  12.1 0.0 copy-start.4
  12.1 0.7 copy-done.4
  12.8 0.0 copy-start.5
  12.8 0.7 copy-done.5
  13.4 0.0 copy-start.6
  13.4 0.7 copy-done.6
  14.1 177.6 %shard_map.149 = (bf16[2,2,8192]{2,1,0:T(2,128)(2,1)S(1)}, f32[8,64,256]{2,1,0:T(8,128)S(1)}) custom-call(bf16[2,2,8192]{2,1,0:T(2,128)(2,1)S(1)} %copy-done.2, f32[16,1,512]{2,1,0:T(1,128)S(1)} %bitcast.17, bf16[16,512,512]{2,1,0:T(8,128)(2,1)} %bitcast.18, bf16[16,512,128]{2,1,0:T(8,128)(2,1)S(1)} %bitcast.13, bf16[16,512,8]{2,1,0:T(8,128)(2,1)S(1)} %bitcast.12, ...), custom_call_target="tpu_custom_call" | custom-call | tf_op jit(solution)/shard_map/pallas_call | solution.py:457
  191.7 0.6 copy.26
  192.3 0.8 copy.27
  (1 shorter events, 0.0 us)
Async XLA Ops:
  7.9 1.6 copy-start
  9.5 1.0 copy-start.1
  10.5 0.8 copy-start.2
  11.4 0.8 copy-start.3
  12.1 0.7 copy-start.4
  12.8 0.7 copy-start.5
  13.4 0.7 copy-start.6

commit v2 on v1

--- a/solution.py
+++ b/solution.py
@@ -14,6 +14,9 @@
 F32 = jnp.float32
 BF16 = jnp.bfloat16
 AHEAD = 3
+BEFORE = 6
+LEAD = 4
+STRIDE = 7
 
 
 def dot(a, b, dims=((1,), (0,)), precision=None):
@@ -27,19 +30,32 @@
 def section(
     sizes,
     hid,
-    gain,
     w_x,
     w_bc,
     w_dt,
     w_out,
     ssm_in,
-    taps,
-    tails,
+    conv_x_in,
+    conv_bc_in,
+    tail_x_in,
+    tail_bc_in,
+    dt_bias_in,
+    a_rate_in,
+    d_skip_in,
+    gain_in,
+    out,
+    state,
+    gain,
     dt_bias,
     a_rate,
     d_skip,
-    out,
-    state,
+    conv_x,
+    conv_bc,
+    tail_x,
+    tail_bc,
+    bc_rows,
+    taps,
+    scaled_v,
     wx_v,
     wbd_v,
     wdt_v,
@@ -81,6 +97,7 @@
     out_s,
     out_r,
     own_s,
+    first_o,
 ):
     n_pipe, n_head, n_x, n_y = sizes
     n_chip = n_head // 2
@@ -102,9 +119,11 @@
     sibling = chip * 2 + 1 - core
 
     def ahead(t):
+        t = lax.rem(t * STRIDE, n_chip)
         return lax.rem(chip_y + lax.div(t, n_x), n_y) * n_x + lax.rem(chip_x + lax.rem(t, n_x), n_x)
 
     def behind(t):
+        t = lax.rem(t * STRIDE, n_chip)
         return lax.rem(chip_y + n_y - lax.div(t, n_x), n_y) * n_x + lax.rem(
             chip_x + n_x - lax.rem(t, n_x), n_x
         )
@@ -129,17 +148,20 @@
 
         lax.fori_loop(first, last, step, 0)
 
-    def load_in(k):
-        pltpu.make_async_copy(w_x.at[k], wx_v.at[k], load_sem.at[0]).start()
-        pltpu.make_async_copy(w_bc.at[k], wbd_v.at[k, :, pl.ds(0, bc_cols)], load_sem.at[1]).start()
-
-    each(0, n_chip, load_in)
-    pltpu.make_async_copy(w_dt, wdt_v, load_sem.at[2]).start()
-    pltpu.make_async_copy(ssm_in, ssm_v, load_sem.at[3]).start()
-    for k in range(n_head):
-        pltpu.make_async_copy(
-            w_out.at[:, pl.ds(k * chunk, chunk)], wo_v.at[k], load_sem.at[4]
-        ).start()
+    small = (
+        (gain_in, gain),
+        (dt_bias_in, dt_bias),
+        (a_rate_in, a_rate),
+        (d_skip_in, d_skip),
+        (conv_x_in, conv_x),
+        (conv_bc_in, conv_bc),
+        (tail_x_in, tail_x),
+        (tail_bc_in, tail_bc),
+        (w_dt, wdt_v),
+        (ssm_in, ssm_v),
+    )
+    for k, (src, dst) in enumerate(small):
+        pltpu.make_async_copy(src, dst, load_sem.at[3 + k]).start()
 
     barrier = pltpu.get_barrier_semaphore()
 
@@ -156,40 +178,80 @@
         pl.semaphore_signal(
             barrier, inc=1, device_id={"pipe": other, "head": me}, device_id_type=MESH
         )
+    def load_in(k):
+        pltpu.make_async_copy(w_x.at[k], wx_v.at[k], load_sem.at[0]).start()
+        pltpu.make_async_copy(w_bc.at[k], wbd_v.at[k, :, pl.ds(0, bc_cols)], load_sem.at[1]).start()
+
+    each(0, n_chip, load_in)
+
+    for k, (src, dst) in enumerate(small):
+        drain(dst, load_sem.at[3 + k])
+
+    bc_all = conv_bc.shape[1]
+    wide_k = 128 * GROUPS
+    spans = bc_all // wide_k
+    bc_rows[...] = jnp.zeros_like(bc_rows)
+    bc_rows[0:4, :] = conv_bc[...]
+    for k in range(3):
+        bc_rows[4 + k : 5 + k, :] = tail_bc[k]
+    pick_row = lax.broadcasted_iota(jnp.int32, (wide_k, 128), 0)
+    pick_col = lax.broadcasted_iota(jnp.int32, (wide_k, 128), 1)
+    pick = jnp.where(pick_row == pick_col * GROUPS + lax.div(me, per_group), 1.0, 0.0)
+    spread_rows = jnp.concatenate(
+        [bc_rows[:, k * wide_k : (k + 1) * wide_k] for k in range(spans)], axis=0
+    )
+    picked = exact(spread_rows, pick)
+    taps[0:4, 0:inner] = conv_x[...]
+    for k in range(3):
+        taps[4 + k : 5 + k, 0:inner] = tail_x[k]
+    for k in range(spans):
+        taps[:, inner + k * 128 : inner + (k + 1) * 128] = picked[k * 8 : (k + 1) * 8]
+    padded[5:8, :] = taps[4:7, :]
+
+    dt_f = wdt_v[...].astype(F32)
+    dt_cols = (
+        jnp.concatenate([dt_f[:, k * 2 * chunk : (k + 1) * 2 * chunk] for k in range(n_chip)], axis=0)
+        .T.astype(BF16)
+        .astype(F32)
+    )
+    dt_at = lax.div(lax.broadcasted_iota(jnp.int32, dt_cols.shape, 1), heads)
+
+    def join(k):
+        wbd_v[k, :, bc_cols : bc_cols + 128] = jnp.where(dt_at == k, dt_cols, 0.0).astype(BF16)
+
+    each(0, n_chip, join)
+    ssm_t[...] = ssm_v[...].reshape(heads * HEAD_DIM, STATE).T
     pl.semaphore_wait(barrier, n_head + 1)
 
-    @pl.when(z == 0)
-    def _():
-        for m in range(micro):
-
-            def give(t):
-                to = lax.rem(me + t, n_head)
-                remote(
-                    hid.at[m, :, pl.ds(pl.multiple_of(to * chunk, chunk), chunk)],
-                    first_in.at[m, me],
-                    first_s.at[m],
-                    first_r.at[m],
-                    to,
-                ).start()
-
-            each(1, n_head, give)
-            pltpu.make_async_copy(
-                hid.at[m, :, pl.ds(pl.multiple_of(me * chunk, chunk), chunk)],
+    def turn(m):
+        def give(t):
+            to = lax.rem(me + t, n_head)
+            remote(
+                hid.at[m, :, pl.ds(pl.multiple_of(to * chunk, chunk), chunk)],
                 first_in.at[m, me],
-                own_s,
+                first_s.at[m],
+                first_r.at[m],
+                to,
             ).start()
-            drain(first_in.at[m, 0], own_s)
+
+        each(1, n_head, give)
+        pltpu.make_async_copy(
+            hid.at[m, :, pl.ds(pl.multiple_of(me * chunk, chunk), chunk)],
+            first_in.at[m, me],
+            first_o.at[m],
+        ).start()
 
     def spread(m):
         mine = h_all.at[m, me]
 
         def give(t):
-            remote(mine, mine, ag_s, ag_r.at[m, t], ahead(t) * 2 + core).start()
+            remote(mine, mine, ag_s.at[m], ag_r.at[m, t], ahead(t) * 2 + core).start()
 
         each(1, n_chip, give)
-        remote(mine, mine, ag_s, fwd_r.at[m, 0], sibling).start()
+        remote(mine, mine, ag_s.at[m], fwd_r.at[m, 0], sibling).start()
 
     def begin(m):
+        drain(first_in.at[m, 0], first_o.at[m])
         drain(first_in.at[m, pl.ds(0, n_head - 1)], first_r.at[m])
         for i in range(n_head):
             total[pl.ds(i * rows, rows), :] = first_in[m, i].astype(F32)
@@ -198,39 +260,37 @@
 
     @pl.when(z == 0)
     def _():
+        turn(0)
         begin(0)
-
-    drain(wdt_v, load_sem.at[2])
-    for_pad = jnp.zeros((2 * chunk, 256 - bc_cols - heads), BF16)
-
-    def join(k):
-        wbd_v[k, :, bc_cols:256] = jnp.concatenate([wdt_v[k], for_pad], axis=1)
-
-    each(0, n_chip, join)
-    drain(ssm_v, load_sem.at[3])
-    ssm_t[...] = ssm_v[...].reshape(heads * HEAD_DIM, STATE).T
-    padded[5:8, :] = tails[...]
+        for m in range(1, micro):
+            turn(m)
+
+    for k in range(n_head):
+        pltpu.make_async_copy(
+            w_out.at[:, pl.ds(k * chunk, chunk)], wo_v.at[k], load_sem.at[2]
+        ).start()
     drain(wx_v, load_sem.at[0])
     drain(wbd_v.at[:, :, pl.ds(0, bc_cols)], load_sem.at[1])
 
+    def carry_on(m):
+        remote(passed.at[m], h_all.at[m, me], pass_s, pass_r.at[m], me).wait_recv()
+        spread(m)
+
+    @pl.when(z > 0)
+    def _():
+        carry_on(0)
+
     def block(m):
-        @pl.when(jnp.logical_and(z == 0, m > 0))
-        def _():
-            begin(m)
-
-        @pl.when(z > 0)
-        def _():
-            remote(passed.at[m], h_all.at[m, me], pass_s, pass_r.at[m], me).wait_recv()
-            spread(m)
+        more = m < micro - 1
 
         acc[...] = jnp.zeros_like(acc)
         squares[...] = jnp.zeros_like(squares)
 
         def relay(t):
             got = h_all.at[m, behind(t) * 2 + core]
-            copy = remote(got, got, ag_s, ag_r.at[m, t], sibling)
+            copy = remote(got, got, ag_s.at[m], ag_r.at[m, t], sibling)
             copy.wait_recv()
-            remote(got, got, ag_s, fwd_r.at[m, t], sibling).start()
+            remote(got, got, ag_s.at[m], fwd_r.at[m, t], sibling).start()
 
         each(1, 1 + AHEAD, relay)
 
@@ -241,7 +301,7 @@
 
             src = behind(t)
             theirs = h_all.at[m, src * 2 + 1 - core]
-            remote(theirs, theirs, ag_s, fwd_r.at[m, t], sibling).wait_recv()
+            remote(theirs, theirs, ag_s.at[m], fwd_r.at[m, t], sibling).wait_recv()
             values = jnp.concatenate([h_all[m, src * 2], h_all[m, src * 2 + 1]], axis=1).astype(F32)
             sq = values * values
             part = sq[:, 0:128]
@@ -249,10 +309,17 @@
                 part = part + sq[:, k * 128 : (k + 1) * 128]
             squares[...] += part
             scaled = (values * gain[src]).astype(BF16)
-            acc[:, 0:inner] += dot(scaled, wx_v[src])
             acc[:, inner : inner + 256] += dot(scaled, wbd_v[src])
-
-        each(0, n_chip, project)
+            return scaled
+
+        def project_both(t):
+            acc[:, 0:inner] += dot(project(t), wx_v[behind(t)])
+
+        def project_later(t):
+            scaled_v[t] = project(t)
+
+        each(0, BEFORE, project_both)
+        each(BEFORE, n_chip, project_later)
         inv = lax.rsqrt(jnp.sum(squares[...], axis=1, keepdims=True) / width + 1e-05)
 
         bc_dt = acc[:, inner : inner + 256] * inv
@@ -274,6 +341,15 @@
         each(1, n_head, give_bc)
         bc_recv[m, me] = bc_send[lax.div(me, per_group)]
 
+        @pl.when(jnp.logical_and(z == 0, more))
+        def _():
+            begin(m + 1)
+
+
+        def finish(t):
+            acc[:, 0:inner] += dot(scaled_v[t], wx_v[behind(t)])
+
+        each(BEFORE, n_chip, finish)
         padded[8 : 8 + tokens, 0:inner] = acc[:, 0:inner] * inv
 
         def conv(lo, hi):
@@ -283,7 +359,10 @@
             return summed * lax.logistic(summed)
 
         x = conv(0, inner)
-        raw = bc_dt[:, bc_cols : bc_cols + heads] + dt_bias[...]
+        fold_row = lax.broadcasted_iota(jnp.int32, (128, heads), 0)
+        fold_col = lax.broadcasted_iota(jnp.int32, (128, heads), 1)
+        fold = jnp.where(lax.rem(fold_row, heads) == fold_col, 1.0, 0.0)
+        raw = exact(bc_dt[:, bc_cols : bc_cols + 128], fold) + dt_bias[...]
         step = jnp.maximum(raw, 0.0) + jnp.log1p(jnp.exp(-jnp.abs(raw)))
         tri_row = lax.broadcasted_iota(jnp.int32, (tokens, tokens), 0)
         tri_col = lax.broadcasted_iota(jnp.int32, (tokens, tokens), 1)
@@ -330,24 +409,24 @@
 
         @pl.when(m == 0)
         def _():
-            drain(wo_v, load_sem.at[4])
+            drain(wo_v, load_sem.at[2])
 
         def for_sibling(i):
             t = lax.rem(i + 1, n_chip)
             sib_send[t] = dot(y_v[...], wo_v[ahead(t) * 2 + 1 - core]).astype(BF16)
             remote(sib_send.at[t], sib_recv.at[m, t], sib_s, sib_r.at[m, t], sibling).start()
 
-        each(0, n_chip, for_sibling)
-
-        def chip_sum(t):
-            part = dot(y_v[...], wo_v[ahead(t) * 2 + core]).astype(BF16).astype(F32)
+        def product(t):
+            return dot(y_v[...], wo_v[ahead(t) * 2 + core]).astype(BF16).astype(F32)
+
+        def chip_sum(t, part):
             remote(
                 sib_send.at[t], sib_recv.at[m, t], sib_s, sib_r.at[m, t], sibling
             ).wait_recv()
             return part + sib_recv[m, t].astype(F32)
 
-        def for_owner(t):
-            sum_send[t] = chip_sum(t).astype(BF16)
+        def for_owner(t, part):
+            sum_send[t] = chip_sum(t, part).astype(BF16)
             remote(
                 sum_send.at[t],
                 sum_recv.at[m, t],
@@ -356,8 +435,16 @@
                 ahead(t) * 2 + core,
             ).start()
 
-        each(1, n_chip, for_owner)
-        total[...] = chip_sum(0) + h_all[m, me].astype(F32)
+        def for_both(i):
+            part = product(i + 1)
+            for_sibling(i + LEAD)
+            for_owner(i + 1, part)
+
+        each(0, LEAD, for_sibling)
+        each(0, n_chip - LEAD, for_both)
+        for t in range(n_chip - LEAD + 1, n_chip):
+            for_owner(t, product(t))
+        total[...] = chip_sum(0, product(0)) + h_all[m, me].astype(F32)
 
         ssm_t[...] = decay_end[0:1, :] * ssm_t[...] + dot(b_end[...], x_end[...], ((0,), (0,)))
 
@@ -377,6 +464,10 @@
         @pl.when(z < n_pipe - 1)
         def _():
             remote(passed.at[m], h_all.at[m, me], pass_s, pass_r.at[m], me, z + 1).start()
+
+        @pl.when(jnp.logical_and(z > 0, more))
+        def _():
+            carry_on(m + 1)
 
         for i in range(n_head):
             out_send[m, i] = total[pl.ds(i * rows, rows), :].astype(BF16)
@@ -399,7 +490,7 @@
         ).start()
 
         drain(out_send.at[m, 0], own_s)
-        drain(h_all.at[m, pl.ds(0, n_head - 1)], ag_s)
+        drain(h_all.at[m, pl.ds(0, n_head - 1)], ag_s.at[m])
         drain(bc_recv.at[m, pl.ds(0, n_head - 1)], bc_s)
         drain(sib_send, sib_s)
         drain(sum_send.at[pl.ds(1, n_chip - 1)], sum_s)
@@ -443,16 +534,8 @@
     inner = w_x.shape[2]
     heads = dt_bias.shape[1]
     bc_cols = w_bc.shape[2]
-    group = lax.axis_index("head") // (n_head // GROUPS)
-
-    def own_group(values):
-        split = values[0].reshape(values.shape[1], -1, GROUPS)
-        return lax.dynamic_index_in_dim(split, group, 2, keepdims=False)
-
-    taps = jnp.concatenate([conv_x[0], own_group(conv_bc)], axis=1)
-    tails = jnp.concatenate([conv_x_init[0], own_group(conv_bc_init)], axis=1)
     vmem = pl.BlockSpec(memory_space=pltpu.VMEM)
-    far = pl.BlockSpec(memory_space=pl.ANY)
+    far = pl.BlockSpec(memory_space=pltpu.HBM)
     dma = pltpu.SemaphoreType.DMA
     out, state = pl.pallas_call(
         functools.partial(section, sizes),
@@ -460,12 +543,23 @@
             jax.ShapeDtypeStruct((micro, rows, width), BF16),
             jax.ShapeDtypeStruct(ssm_init.shape[1:], F32),
         ),
-        in_specs=[vmem, vmem, far, far, far, far, far, vmem, vmem, vmem, vmem, vmem],
+        in_specs=[far] * 14,
         out_specs=(vmem, vmem),
         scratch_shapes=[
+            pltpu.VMEM((n_chip, 1, 2 * chunk), F32),
+            pltpu.VMEM((1, heads), F32),
+            pltpu.VMEM((1, heads), F32),
+            pltpu.VMEM((1, heads), F32),
+            pltpu.VMEM(conv_x.shape[1:], F32),
+            pltpu.VMEM(conv_bc.shape[1:], F32),
+            pltpu.VMEM((conv_x_init.shape[1], 1, conv_x_init.shape[2]), F32),
+            pltpu.VMEM((conv_bc_init.shape[1], 1, conv_bc_init.shape[2]), F32),
+            pltpu.VMEM((8, conv_bc.shape[2]), F32),
+            pltpu.VMEM((8, inner + 2 * STATE), F32),
+            pltpu.VMEM((n_chip, tokens, 2 * chunk), BF16),
             pltpu.VMEM((n_chip, 2 * chunk, inner), BF16),
             pltpu.VMEM((n_chip, 2 * chunk, 256), BF16),
-            pltpu.VMEM((n_chip, 2 * chunk, heads), BF16),
+            pltpu.VMEM((heads, width), BF16),
             pltpu.VMEM((n_head, inner, chunk), BF16),
             pltpu.VMEM(ssm_init.shape[1:], F32),
             pltpu.VMEM((STATE, inner), F32),
@@ -487,10 +581,10 @@
             pltpu.VMEM((tokens, chunk), F32),
             pltpu.VMEM((micro, tokens, chunk), BF16),
             pltpu.VMEM((micro, n_head, rows, chunk), BF16),
-            dma((5,)),
+            dma((13,)),
             dma((micro,)),
             dma((micro,)),
-            dma,
+            dma((micro,)),
             dma((micro, n_chip)),
             dma((micro, n_chip)),
             dma,
@@ -504,23 +598,31 @@
             dma,
             dma((micro,)),
             dma,
+            dma((micro,)),
         ],
         compiler_params=pltpu.CompilerParams(
             collective_id=0, has_side_effects=True, vmem_limit_bytes=48 << 20
         ),
     )(
-        hidden,
-        norm_gain.reshape(n_chip, 1, 2 * chunk),
-        w_x.reshape(n_chip, 2 * chunk, inner),
-        w_bc.reshape(n_chip, 2 * chunk, bc_cols),
-        w_dt.reshape(n_chip, 2 * chunk, heads),
-        w_out[0],
-        ssm_init[0],
-        taps,
-        tails,
-        dt_bias,
-        a_rate,
-        d_skip,
+        *(
+            pltpu.with_memory_space_constraint(value, pltpu.HBM)
+            for value in (
+                hidden,
+                w_x.reshape(n_chip, 2 * chunk, inner),
+                w_bc.reshape(n_chip, 2 * chunk, bc_cols),
+                w_dt[0].T,
+                w_out[0],
+                ssm_init[0],
+                conv_x[0],
+                conv_bc[0],
+                conv_x_init.transpose(1, 0, 2),
+                conv_bc_init.transpose(1, 0, 2),
+                dt_bias,
+                a_rate,
+                d_skip,
+                norm_gain.reshape(n_chip, 1, 2 * chunk),
+            )
+        )
     )
     return (out[None], state[None])
 

time: 194 us -> 163 us (0.84)
  Pallas kernels: 178 us -> 161 us
  local copies, waits for them, and re-layouts: 13.2 us -> 1.42 us
    pallas_call x1, Pallas kernels: 178 us -> 161 us  [per_device(): pl.pallas_call(functools.partial(section, sizes), out_shape=(jax.ShapeDty...]
    unnamed x18 -> x2, local copies, waits for them, and re-layouts: 10.1 us -> 1.42 us
where the time goes in v2:
time: 163 us
  Pallas kernels  161 us (99%)
    pallas_call x1, Pallas kernels, per_device(): pl.pallas_call(functools.partial(section, sizes), out_shape=(jax.ShapeDty...  161 us

profile of v2, /device:TPU:97, one launch (start us, length us, event | category | flops | bytes accessed | tf_op | source)
XLA Modules:
  0.0 163.2 jit_solution(4092397085232724581)
XLA Ops:
  0.6 161.1 %shard_map.149 = (bf16[2,2,8192]{2,1,0:T(2,128)(2,1)S(1)}, f32[8,64,256]{2,1,0:T(8,128)S(1)}) custom-call(bf16[2,2,8192]{2,1,0:T(2,128)(2,1)} %hid.1, bf16[16,512,512]{2,1,0:T(8,128)(2,1)} %bitcast.16, bf16[16,512,128]{2,1,0:T(8,128)(2,1)} %bitcast.18, bf16[8,8192]{1,0:T(8,128)(2,1)} %bitcast.20, bf16[512,8192]{1,0:T(8,128)(2,1)} %bitcast.17, ...), custom_call_target="tpu_custom_call" | custom-call | tf_op jit(solution)/shard_map/pallas_call | solution.py:540
  161.8 0.6 copy.18
  162.4 0.8 copy.19

commit v3 on v2

--- a/solution.py
+++ b/solution.py
@@ -13,10 +13,14 @@
 MESH = pl.DeviceIdType.MESH
 F32 = jnp.float32
 BF16 = jnp.bfloat16
-AHEAD = 3
+AHEAD = 4
+EARLY = 7
 BEFORE = 6
 LEAD = 4
-STRIDE = 7
+SIDE = 4
+NEAR = (2, 8, 1, 4, 3, 12, 5, 7, 13, 15)
+ORDER = (0, 1, 4, 3, 12, 2, 8, 5, 7, 13, 15, 6, 14, 9, 11, 10)
+HANDED = {2: (4, 12, 8), 8: (1, 3)}
 
 
 def dot(a, b, dims=((1,), (0,)), precision=None):
@@ -119,14 +123,21 @@
     sibling = chip * 2 + 1 - core
 
     def ahead(t):
-        t = lax.rem(t * STRIDE, n_chip)
         return lax.rem(chip_y + lax.div(t, n_x), n_y) * n_x + lax.rem(chip_x + lax.rem(t, n_x), n_x)
 
     def behind(t):
-        t = lax.rem(t * STRIDE, n_chip)
         return lax.rem(chip_y + n_y - lax.div(t, n_x), n_y) * n_x + lax.rem(
             chip_x + n_x - lax.rem(t, n_x), n_x
         )
+
+    def nearest(t):
+        value = ORDER[0] + 0 * t
+        for k in range(1, n_chip):
+            value = value + (ORDER[k] - ORDER[k - 1]) * lax.div(t + n_chip - k, n_chip)
+        return value
+
+    def mixed(t):
+        return ahead(nearest(lax.rem(n_chip - t, n_chip)))
 
     def remote(src, dst, send, recv, head, pipe=None):
         return pltpu.make_async_remote_copy(
@@ -244,10 +255,8 @@
     def spread(m):
         mine = h_all.at[m, me]
 
-        def give(t):
-            remote(mine, mine, ag_s.at[m], ag_r.at[m, t], ahead(t) * 2 + core).start()
-
-        each(1, n_chip, give)
+        for u in NEAR:
+            remote(mine, mine, ag_s.at[m], ag_r.at[m, u], ahead(u) * 2 + core).start()
         remote(mine, mine, ag_s.at[m], fwd_r.at[m, 0], sibling).start()
 
     def begin(m):
@@ -286,22 +295,26 @@
         acc[...] = jnp.zeros_like(acc)
         squares[...] = jnp.zeros_like(squares)
 
-        def relay(t):
-            got = h_all.at[m, behind(t) * 2 + core]
-            copy = remote(got, got, ag_s.at[m], ag_r.at[m, t], sibling)
+        def relay(u, handed=()):
+            got = h_all.at[m, behind(u) * 2 + core]
+            copy = remote(got, got, ag_s.at[m], ag_r.at[m, u], sibling)
             copy.wait_recv()
-            remote(got, got, ag_s.at[m], fwd_r.at[m, t], sibling).start()
-
-        each(1, 1 + AHEAD, relay)
+            for v in handed:
+                remote(got, got, ag_s.at[m], ag_r.at[m, u + v], ahead(v) * 2 + core).start()
+            remote(got, got, ag_s.at[m], fwd_r.at[m, u], sibling).start()
+
+        for u in ORDER[1:EARLY]:
+            relay(u, HANDED.get(u, ()))
 
         def project(t):
-            @pl.when(t + 1 + AHEAD < n_chip)
+            @pl.when(jnp.logical_and(t + AHEAD >= EARLY, t + AHEAD < n_chip))
             def _():
-                relay(t + 1 + AHEAD)
-
-            src = behind(t)
+                relay(nearest(t + AHEAD))
+
+            u = nearest(t)
+            src = behind(u)
             theirs = h_all.at[m, src * 2 + 1 - core]
-            remote(theirs, theirs, ag_s.at[m], fwd_r.at[m, t], sibling).wait_recv()
+            remote(theirs, theirs, ag_s.at[m], fwd_r.at[m, u], sibling).wait_recv()
             values = jnp.concatenate([h_all[m, src * 2], h_all[m, src * 2 + 1]], axis=1).astype(F32)
             sq = values * values
             part = sq[:, 0:128]
@@ -313,7 +326,7 @@
             return scaled
 
         def project_both(t):
-            acc[:, 0:inner] += dot(project(t), wx_v[behind(t)])
+            acc[:, 0:inner] += dot(project(t), wx_v[behind(nearest(t))])
 
         def project_later(t):
             scaled_v[t] = project(t)
@@ -330,16 +343,16 @@
         width_n = bc_cols // GROUPS
         wanted = lax.rem(at_row, width_n) * GROUPS + lax.div(at_row, width_n)
         order = jnp.where(at_col == wanted, 1.0, 0.0).astype(BF16)
-        bc_send[...] = dot(order, bc_wide, ((1,), (1,))).astype(BF16).reshape(bc_send.shape)
+        bc_send[m] = dot(order, bc_wide, ((1,), (1,))).astype(BF16).reshape(bc_send.shape[1:])
 
         def give_bc(t):
             to = lax.rem(me + t, n_head)
             remote(
-                bc_send.at[lax.div(to, per_group)], bc_recv.at[m, me], bc_s, bc_r.at[m], to
+                bc_send.at[m, lax.div(to, per_group)], bc_recv.at[m, me], bc_s, bc_r.at[m], to
             ).start()
 
         each(1, n_head, give_bc)
-        bc_recv[m, me] = bc_send[lax.div(me, per_group)]
+        bc_recv[m, me] = bc_send[m, lax.div(me, per_group)]
 
         @pl.when(jnp.logical_and(z == 0, more))
         def _():
@@ -347,7 +360,7 @@
 
 
         def finish(t):
-            acc[:, 0:inner] += dot(scaled_v[t], wx_v[behind(t)])
+            acc[:, 0:inner] += dot(scaled_v[t], wx_v[behind(nearest(t))])
 
         each(BEFORE, n_chip, finish)
         padded[8 : 8 + tokens, 0:inner] = acc[:, 0:inner] * inv
@@ -413,26 +426,26 @@
 
         def for_sibling(i):
             t = lax.rem(i + 1, n_chip)
-            sib_send[t] = dot(y_v[...], wo_v[ahead(t) * 2 + 1 - core]).astype(BF16)
-            remote(sib_send.at[t], sib_recv.at[m, t], sib_s, sib_r.at[m, t], sibling).start()
+            sib_send[m, t] = dot(y_v[...], wo_v[mixed(t) * 2 + 1 - core]).astype(BF16)
+            remote(sib_send.at[m, t], sib_recv.at[m, t], sib_s, sib_r.at[m, t], sibling).start()
 
         def product(t):
-            return dot(y_v[...], wo_v[ahead(t) * 2 + core]).astype(BF16).astype(F32)
+            return dot(y_v[...], wo_v[mixed(t) * 2 + core]).astype(BF16).astype(F32)
 
         def chip_sum(t, part):
             remote(
-                sib_send.at[t], sib_recv.at[m, t], sib_s, sib_r.at[m, t], sibling
+                sib_send.at[m, t], sib_recv.at[m, t], sib_s, sib_r.at[m, t], sibling
             ).wait_recv()
             return part + sib_recv[m, t].astype(F32)
 
         def for_owner(t, part):
-            sum_send[t] = chip_sum(t, part).astype(BF16)
+            sum_send[m, t] = chip_sum(t, part).astype(BF16)
             remote(
-                sum_send.at[t],
+                sum_send.at[m, t],
                 sum_recv.at[m, t],
                 sum_s,
                 sum_r.at[m, t],
-                ahead(t) * 2 + core,
+                mixed(t) * 2 + core,
             ).start()
 
         def for_both(i):
@@ -454,7 +467,7 @@
 
         def take(t):
             remote(
-                sum_send.at[t], sum_recv.at[m, t], sum_s, sum_r.at[m, t], sibling
+                sum_send.at[m, t], sum_recv.at[m, t], sum_s, sum_r.at[m, t], sibling
             ).wait_recv()
             total[...] += sum_recv[m, t].astype(F32)
 
@@ -486,27 +499,29 @@
         pltpu.make_async_copy(
             out_send.at[m, me],
             out.at[m, :, pl.ds(pl.multiple_of(me * chunk, chunk), chunk)],
-            own_s,
+            own_s.at[m],
         ).start()
 
-        drain(out_send.at[m, 0], own_s)
+    each(0, micro, block)
+    def settle(m):
+        drain(out_send.at[m, 0], own_s.at[m])
         drain(h_all.at[m, pl.ds(0, n_head - 1)], ag_s.at[m])
         drain(bc_recv.at[m, pl.ds(0, n_head - 1)], bc_s)
-        drain(sib_send, sib_s)
-        drain(sum_send.at[pl.ds(1, n_chip - 1)], sum_s)
+        drain(sib_send.at[m], sib_s)
+        drain(sum_send.at[m, pl.ds(1, n_chip - 1)], sum_s)
         drain(out_send.at[m, pl.ds(0, n_head - 1)], out_s)
 
         @pl.when(z < n_pipe - 1)
         def _():
-            remote(passed.at[m], h_all.at[m, me], pass_s, pass_r.at[m], me).wait_send()
+            drain(passed.at[m], pass_s)
 
         @pl.when(z == 0)
         def _():
             drain(first_in.at[m, pl.ds(0, n_head - 1)], first_s.at[m])
 
-    each(0, micro, block)
-    for m in range(micro):
         drain(out.at[m, :, pl.ds(0, (n_head - 1) * chunk)], out_r.at[m])
+
+    each(0, micro, settle)
 
 
 def per_device(
@@ -568,15 +583,15 @@
             pltpu.VMEM((tokens, inner + 256), F32),
             pltpu.VMEM((tokens, 128), F32),
             pltpu.VMEM((8 + tokens, inner + 2 * STATE), F32),
-            pltpu.VMEM((GROUPS, bc_cols // GROUPS, 128), BF16),
+            pltpu.VMEM((micro, GROUPS, bc_cols // GROUPS, 128), BF16),
             pltpu.VMEM((micro, n_head, bc_cols // GROUPS, 128), BF16),
             pltpu.VMEM((tokens, inner), BF16),
             pltpu.VMEM((tokens, inner), BF16),
             pltpu.VMEM((tokens, STATE), BF16),
             pltpu.VMEM((8, inner), F32),
-            pltpu.VMEM((n_chip, tokens, chunk), BF16),
             pltpu.VMEM((micro, n_chip, tokens, chunk), BF16),
-            pltpu.VMEM((n_chip, tokens, chunk), BF16),
+            pltpu.VMEM((micro, n_chip, tokens, chunk), BF16),
+            pltpu.VMEM((micro, n_chip, tokens, chunk), BF16),
             pltpu.VMEM((micro, n_chip, tokens, chunk), BF16),
             pltpu.VMEM((tokens, chunk), F32),
             pltpu.VMEM((micro, tokens, chunk), BF16),
@@ -597,7 +612,7 @@
             dma((micro,)),
             dma,
             dma((micro,)),
-            dma,
+            dma((micro,)),
             dma((micro,)),
         ],
         compiler_params=pltpu.CompilerParams(
@@ -630,9 +645,7 @@
 def solution(mesh):
     n_pipe = mesh.shape["pipe"]
     n_head = mesh.shape["head"]
-    n_x = 1
-    while n_x * n_x < n_head // 2:
-        n_x *= 2
+    n_x = SIDE
     in_specs = (
         P(None, "head", None),
         P("pipe", None),

time: 163 us -> 159 us (0.975)
  Pallas kernels: 161 us -> 157 us
    pallas_call x1, Pallas kernels: 161 us -> 157 us  [per_device(): pl.pallas_call(functools.partial(section, sizes), out_shape=(jax.ShapeDty...]
where the time goes in v3:
time: 159 us
  Pallas kernels  157 us (99%)
    pallas_call x1, Pallas kernels, per_device(): pl.pallas_call(functools.partial(section, sizes), out_shape=(jax.ShapeDty...  157 us

profile of v3, /device:TPU:97, one launch (start us, length us, event | category | flops | bytes accessed | tf_op | source)
XLA Modules:
  0.0 159.1 jit_solution(17353896724753676219)
XLA Ops:
  0.6 157.0 %shard_map.149 = (bf16[2,2,8192]{2,1,0:T(2,128)(2,1)S(1)}, f32[8,64,256]{2,1,0:T(8,128)S(1)}) custom-call(bf16[2,2,8192]{2,1,0:T(2,128)(2,1)} %hid.1, bf16[16,512,512]{2,1,0:T(8,128)(2,1)} %bitcast.16, bf16[16,512,128]{2,1,0:T(8,128)(2,1)} %bitcast.18, bf16[8,8192]{1,0:T(8,128)(2,1)} %bitcast.20, bf16[512,8192]{1,0:T(8,128)(2,1)} %bitcast.17, ...), custom_call_target="tpu_custom_call" | custom-call | tf_op jit(solution)/shard_map/pallas_call | solution.py:555
  157.6 0.6 copy.18
  158.3 0.8 copy.19

commit v4 on v3

--- a/solution.py
+++ b/solution.py
@@ -19,7 +19,7 @@
 LEAD = 4
 SIDE = 4
 NEAR = (2, 8, 1, 4, 3, 12, 5, 7, 13, 15)
-ORDER = (0, 1, 4, 3, 12, 2, 8, 5, 7, 13, 15, 6, 14, 9, 11, 10)
+ORDER = (0, 2, 8, 1, 4, 3, 12, 5, 7, 13, 15, 6, 14, 9, 11, 10)
 HANDED = {2: (4, 12, 8), 8: (1, 3)}
 
 
@@ -195,6 +195,45 @@
 
     each(0, n_chip, load_in)
 
+    pl.semaphore_wait(barrier, n_head + 1)
+
+    def turn(m):
+        def give(t):
+            to = lax.rem(me + t, n_head)
+            remote(
+                hid.at[m, :, pl.ds(pl.multiple_of(to * chunk, chunk), chunk)],
+                first_in.at[m, me],
+                first_s.at[m],
+                first_r.at[m],
+                to,
+            ).start()
+
+        each(1, n_head, give)
+        pltpu.make_async_copy(
+            hid.at[m, :, pl.ds(pl.multiple_of(me * chunk, chunk), chunk)],
+            first_in.at[m, me],
+            first_o.at[m],
+        ).start()
+
+    def spread(m):
+        mine = h_all.at[m, me]
+
+        for u in NEAR:
+            remote(mine, mine, ag_s.at[m], ag_r.at[m, u], ahead(u) * 2 + core).start()
+        remote(mine, mine, ag_s.at[m], fwd_r.at[m, 0], sibling).start()
+
+    def begin(m):
+        drain(first_in.at[m, 0], first_o.at[m])
+        drain(first_in.at[m, pl.ds(0, n_head - 1)], first_r.at[m])
+        for i in range(n_head):
+            total[pl.ds(i * rows, rows), :] = first_in[m, i].astype(F32)
+        h_all[m, me] = total[...].astype(BF16)
+        spread(m)
+
+    @pl.when(z == 0)
+    def _():
+        turn(0)
+
     for k, (src, dst) in enumerate(small):
         drain(dst, load_sem.at[3 + k])
 
@@ -219,6 +258,14 @@
         taps[:, inner + k * 128 : inner + (k + 1) * 128] = picked[k * 8 : (k + 1) * 8]
     padded[5:8, :] = taps[4:7, :]
 
+    ssm_t[...] = ssm_v[...].reshape(heads * HEAD_DIM, STATE).T
+
+    @pl.when(z == 0)
+    def _():
+        begin(0)
+        for m in range(1, micro):
+            turn(m)
+
     dt_f = wdt_v[...].astype(F32)
     dt_cols = (
         jnp.concatenate([dt_f[:, k * 2 * chunk : (k + 1) * 2 * chunk] for k in range(n_chip)], axis=0)
@@ -231,48 +278,6 @@
         wbd_v[k, :, bc_cols : bc_cols + 128] = jnp.where(dt_at == k, dt_cols, 0.0).astype(BF16)
 
     each(0, n_chip, join)
-    ssm_t[...] = ssm_v[...].reshape(heads * HEAD_DIM, STATE).T
-    pl.semaphore_wait(barrier, n_head + 1)
-
-    def turn(m):
-        def give(t):
-            to = lax.rem(me + t, n_head)
-            remote(
-                hid.at[m, :, pl.ds(pl.multiple_of(to * chunk, chunk), chunk)],
-                first_in.at[m, me],
-                first_s.at[m],
-                first_r.at[m],
-                to,
-            ).start()
-
-        each(1, n_head, give)
-        pltpu.make_async_copy(
-            hid.at[m, :, pl.ds(pl.multiple_of(me * chunk, chunk), chunk)],
-            first_in.at[m, me],
-            first_o.at[m],
-        ).start()
-
-    def spread(m):
-        mine = h_all.at[m, me]
-
-        for u in NEAR:
-            remote(mine, mine, ag_s.at[m], ag_r.at[m, u], ahead(u) * 2 + core).start()
-        remote(mine, mine, ag_s.at[m], fwd_r.at[m, 0], sibling).start()
-
-    def begin(m):
-        drain(first_in.at[m, 0], first_o.at[m])
-        drain(first_in.at[m, pl.ds(0, n_head - 1)], first_r.at[m])
-        for i in range(n_head):
-            total[pl.ds(i * rows, rows), :] = first_in[m, i].astype(F32)
-        h_all[m, me] = total[...].astype(BF16)
-        spread(m)
-
-    @pl.when(z == 0)
-    def _():
-        turn(0)
-        begin(0)
-        for m in range(1, micro):
-            turn(m)
 
     for k in range(n_head):
         pltpu.make_async_copy(
@@ -345,13 +350,18 @@
         order = jnp.where(at_col == wanted, 1.0, 0.0).astype(BF16)
         bc_send[m] = dot(order, bc_wide, ((1,), (1,))).astype(BF16).reshape(bc_send.shape[1:])
 
-        def give_bc(t):
-            to = lax.rem(me + t, n_head)
+        def give_bc(to):
             remote(
                 bc_send.at[m, lax.div(to, per_group)], bc_recv.at[m, me], bc_s, bc_r.at[m], to
             ).start()
 
-        each(1, n_head, give_bc)
+        def give_chip(t):
+            to = mixed(t) * 2
+            give_bc(to + core)
+            give_bc(to + 1 - core)
+
+        each(1, n_chip, give_chip)
+        give_bc(sibling)
         bc_recv[m, me] = bc_send[m, lax.div(me, per_group)]
 
         @pl.when(jnp.logical_and(z == 0, more))
@@ -471,22 +481,22 @@
             ).wait_recv()
             total[...] += sum_recv[m, t].astype(F32)
 
-        each(1, n_chip, take)
+        each(1, n_chip - 5, take)
+        @pl.when(jnp.logical_and(z > 0, more))
+        def _():
+            carry_on(m + 1)
+
+        each(n_chip - 5, n_chip, take)
         passed[m] = total[...].astype(BF16)
 
         @pl.when(z < n_pipe - 1)
         def _():
             remote(passed.at[m], h_all.at[m, me], pass_s, pass_r.at[m], me, z + 1).start()
 
-        @pl.when(jnp.logical_and(z > 0, more))
-        def _():
-            carry_on(m + 1)
-
         for i in range(n_head):
             out_send[m, i] = total[pl.ds(i * rows, rows), :].astype(BF16)
 
-        def give_out(t):
-            to = lax.rem(me + t, n_head)
+        def give_out(to):
             remote(
                 out_send.at[m, to],
                 out.at[m, :, pl.ds(pl.multiple_of(me * chunk, chunk), chunk)],
@@ -495,7 +505,13 @@
                 to,
             ).start()
 
-        each(1, n_head, give_out)
+        def give_out_chip(t):
+            to = mixed(t) * 2
+            give_out(to + core)
+            give_out(to + 1 - core)
+
+        each(1, n_chip, give_out_chip)
+        give_out(sibling)
         pltpu.make_async_copy(
             out_send.at[m, me],
             out.at[m, :, pl.ds(pl.multiple_of(me * chunk, chunk), chunk)],

time: 159 us -> 154 us (0.969)
  Pallas kernels: 157 us -> 152 us
    pallas_call x1, Pallas kernels: 157 us -> 152 us  [per_device(): pl.pallas_call(functools.partial(section, sizes), out_shape=(jax.ShapeDty...]
where the time goes in v4:
time: 154 us
  Pallas kernels  152 us (99%)
    pallas_call x1, Pallas kernels, per_device(): pl.pallas_call(functools.partial(section, sizes), out_shape=(jax.ShapeDty...  152 us

profile of v4, /device:TPU:97, one launch (start us, length us, event | category | flops | bytes accessed | tf_op | source)
XLA Modules:
  0.0 154.3 jit_solution(9099655576330927539)
XLA Ops:
  0.6 152.2 %shard_map.149 = (bf16[2,2,8192]{2,1,0:T(2,128)(2,1)S(1)}, f32[8,64,256]{2,1,0:T(8,128)S(1)}) custom-call(bf16[2,2,8192]{2,1,0:T(2,128)(2,1)} %hid.1, bf16[16,512,512]{2,1,0:T(8,128)(2,1)} %bitcast.16, bf16[16,512,128]{2,1,0:T(8,128)(2,1)} %bitcast.18, bf16[8,8192]{1,0:T(8,128)(2,1)} %bitcast.20, bf16[512,8192]{1,0:T(8,128)(2,1)} %bitcast.17, ...), custom_call_target="tpu_custom_call" | custom-call | tf_op jit(solution)/shard_map/pallas_call | solution.py:571
  152.8 0.6 copy.18
  153.5 0.8 copy.19

commit v5 on v4

--- a/solution.py
+++ b/solution.py
@@ -481,12 +481,12 @@
             ).wait_recv()
             total[...] += sum_recv[m, t].astype(F32)
 
-        each(1, n_chip - 5, take)
+        each(1, n_chip - 8, take)
         @pl.when(jnp.logical_and(z > 0, more))
         def _():
             carry_on(m + 1)
 
-        each(n_chip - 5, n_chip, take)
+        each(n_chip - 8, n_chip, take)
         passed[m] = total[...].astype(BF16)
 
         @pl.when(z < n_pipe - 1)

time: 154 us -> 154 us (level)
  no operation moved by 1% of the time
where the time goes in v5:
time: 154 us
  Pallas kernels  152 us (99%)
    pallas_call x1, Pallas kernels, per_device(): pl.pallas_call(functools.partial(section, sizes), out_shape=(jax.ShapeDty...  152 us

profile of v5, /device:TPU:97, one launch (start us, length us, event | category | flops | bytes accessed | tf_op | source)
XLA Modules:
  0.0 153.9 jit_solution(16258683765163286206)
XLA Ops:
  0.6 151.9 %shard_map.149 = (bf16[2,2,8192]{2,1,0:T(2,128)(2,1)S(1)}, f32[8,64,256]{2,1,0:T(8,128)S(1)}) custom-call(bf16[2,2,8192]{2,1,0:T(2,128)(2,1)} %hid.1, bf16[16,512,512]{2,1,0:T(8,128)(2,1)} %bitcast.16, bf16[16,512,128]{2,1,0:T(8,128)(2,1)} %bitcast.18, bf16[8,8192]{1,0:T(8,128)(2,1)} %bitcast.20, bf16[512,8192]{1,0:T(8,128)(2,1)} %bitcast.17, ...), custom_call_target="tpu_custom_call" | custom-call | tf_op jit(solution)/shard_map/pallas_call | solution.py:571
  152.5 0.6 copy.18
  153.2 0.8 copy.19
